TPU v7x, 128 devices: a whole 4x4x4 slice. The times are simulated.
128 devices in a mesh: lat: 8 (over x, core), lon: 16 (over z, y).
Axes of the slice: x: 4, y: 4, z: 4, core: 2. Of those that a mesh axis runs over, the one named last changes fastest.
Arguments:
- obs_value: float32 [128, 21, 128, 128], P(('lat', 'lon')), may hold values from -6 to 6
- obs_cell: int32 [128, 128, 128], P(('lat', 'lon')), may hold values from 0 to 12287
- obs_count: int32 [128, 128], P(('lat', 'lon')), may hold values from 0 to 128, as said below
- bottom_level: int32 [384, 4096], P('lat', 'lon'), may hold values from 0 to 10
- diffusivity: float32 [2, 384, 4096], P(None, 'lat', 'lon'), may hold values from 0.5 to 16
- partner: int32 [4096], P('lon'), may hold values from 0 to 4095, as said below
- length_scale: float32 [21], replicated, may hold values from 0.25 to 2
- sigma: float32 [21], replicated, may hold values from 0.5 to 2
Outputs:
- obs_fit: float32 [128, 21, 128, 128], P(('lat', 'lon'))
- diffused: float32 [21, 384, 4096], P(None, 'lat', 'lon')
Inputs may be any that keep to these rules, and one draw needn't show every extreme that they name: `obs_count`: at most 128 live slots from one device to one owner; in every draw one owner receives 128 from every device. partner[i] = (centre - i) mod 4096 for one centre of each draw.
All inputs are finite; a program needn't handle non-finite values.
Results may differ from a plain program's by a relative error of at most 0.00002.
Values sent between devices are 32-bit elements; how exact they have to be, the bound alone decides.
A program may use at most 128 MiB of HBM per device.

v0:
```python
import jax
import jax.numpy as jnp
from jax import lax
from jax.sharding import PartitionSpec as P

LEV = 10
STEPS = 2
SWEEPS = 6


def with_halo(block, sides, width, periodic):
    for axis, dim in sides:
        count = lax.axis_size(axis)
        forward = [(i, i + 1) for i in range(count - 1)]
        if periodic:
            forward.append((count - 1, 0))
        backward = [(target, source) for source, target in forward]
        low = lax.ppermute(
            lax.slice_in_dim(block, block.shape[dim] - width, None, axis=dim), axis, forward
        )
        high = lax.ppermute(lax.slice_in_dim(block, 0, width, axis=dim), axis, backward)
        block = jnp.concatenate([low, block, high], axis=dim)
    return block


def extend_deep(block, depth, partner_wide, top_band):
    tile_rows = block.shape[1]
    sideways = with_halo(block, (("lon", 2),), depth, True)
    extended = with_halo(sideways, (("lat", 1),), depth, False)
    top_rows = lax.all_gather(block[:, tile_rows - depth :, :], "lon", axis=2, tiled=True)
    ghost = jnp.take(top_rows, partner_wide, axis=2)[:, ::-1, :]
    upper = jnp.where(top_band, ghost, extended[:, tile_rows + depth :, :])
    return extended.at[:, tile_rows + depth :, :].set(upper)


def face_weights(coef_pad, channels, scale):
    centre = coef_pad[:, 1:-1, 1:-1]
    wet_mask = centre[:channels]
    kappa_lon = centre[channels][None]
    kappa_lat = centre[channels + 1][None]
    wet_pad = coef_pad[:channels]
    lon_pad = coef_pad[channels][None]
    lat_pad = coef_pad[channels + 1][None]
    w_east = scale * (0.5 * (kappa_lon + lon_pad[:, 1:-1, 2:])) * wet_mask * wet_pad[:, 1:-1, 2:]
    w_west = scale * (0.5 * (kappa_lon + lon_pad[:, 1:-1, :-2])) * wet_mask * wet_pad[:, 1:-1, :-2]
    w_north = scale * (0.5 * (kappa_lat + lat_pad[:, 2:, 1:-1])) * wet_mask * wet_pad[:, 2:, 1:-1]
    w_south = scale * (0.5 * (kappa_lat + lat_pad[:, :-2, 1:-1])) * wet_mask * wet_pad[:, :-2, 1:-1]
    diagonal_sum = 1.0 + w_east + w_west + w_north + w_south
    return (w_east, w_west, w_north, w_south, diagonal_sum)


def trim_margin(array, outer, inner):
    offset = outer - inner
    return array[:, offset : array.shape[1] - offset, offset : array.shape[2] - offset]


def per_device(
    obs_value, obs_cell, obs_count, bottom_level, diffusivity, partner, length_scale, sigma
):
    channels = obs_value.shape[1]
    devices = obs_value.shape[2]
    slots = obs_value.shape[3]
    lat_count = lax.axis_size("lat")
    top_band = lax.axis_index("lat") == lat_count - 1
    level_of = jnp.concatenate(
        [
            jnp.arange(LEV, dtype=jnp.int32),
            jnp.arange(LEV, dtype=jnp.int32),
            jnp.zeros((1,), jnp.int32),
        ]
    )
    wet_mask = (level_of[:, None, None] < bottom_level[None]).astype(jnp.float32)
    live_slots = (jnp.arange(slots, dtype=jnp.int32)[None, :] < obs_count[0][:, None]).astype(
        jnp.float32
    )
    outgoing = obs_value * live_slots[None, None]
    cell_block = obs_cell.reshape(1, 1, devices, slots)
    arrived, cell_ids = (
        lax.all_to_all(outgoing, ("lat", "lon"), split_axis=2, concat_axis=2, tiled=True),
        lax.all_to_all(cell_block, ("lat", "lon"), split_axis=2, concat_axis=2, tiled=True),
    )
    spread = arrived.reshape(channels, -1)
    cell_ids = cell_ids.reshape(-1)
    tile_rows = bottom_level.shape[0]
    tile_cols = bottom_level.shape[1]
    field = jnp.zeros((channels, tile_rows * tile_cols), jnp.float32).at[:, cell_ids].add(spread)
    field = field.reshape(channels, tile_rows, tile_cols) * (sigma[:, None, None] * wet_mask)
    coef_stack = jnp.concatenate([wet_mask, diffusivity], axis=0)
    scale = length_scale[:, None, None]
    state = field
    depth = SWEEPS
    partner_wide = with_halo(partner, (("lon", 0),), depth + 1, True)
    coef_pad = extend_deep(coef_stack, depth + 1, partner_wide, top_band)
    w_east, w_west, w_north, w_south, diagonal_sum = face_weights(coef_pad, channels, scale)
    partner_mid = partner_wide[1:-1]
    for step_index in range(STEPS):
        source_wide = extend_deep(state, depth, partner_mid, top_band)
        current = source_wide
        for sweep_index in range(SWEEPS):
            inner = depth - sweep_index - 1
            current = (
                trim_margin(source_wide, depth, inner)
                + trim_margin(w_east, depth, inner) * current[:, 1:-1, 2:]
                + trim_margin(w_west, depth, inner) * current[:, 1:-1, :-2]
                + trim_margin(w_north, depth, inner) * current[:, 2:, 1:-1]
                + trim_margin(w_south, depth, inner) * current[:, :-2, 1:-1]
            ) / trim_margin(diagonal_sum, depth, inner)
        state = current
    diffused = sigma[:, None, None] * state
    local_fit = diffused.reshape(channels, -1)[:, cell_ids]
    returned = lax.all_to_all(
        local_fit.reshape(1, channels, devices, slots),
        ("lat", "lon"),
        split_axis=2,
        concat_axis=2,
        tiled=True,
    )
    obs_fit = returned * live_slots[None, None]
    return (obs_fit, diffused)


def solution(mesh):
    return jax.shard_map(
        per_device,
        mesh=mesh,
        in_specs=(
            P(("lat", "lon"), None, None, None),
            P(("lat", "lon"), None, None),
            P(("lat", "lon"), None),
            P("lat", "lon"),
            P(None, "lat", "lon"),
            P("lon"),
            P(),
            P(),
        ),
        out_specs=(P(("lat", "lon"), None, None, None), P(None, "lat", "lon")),
        check_vma=False,
    )
```

profile of v0, /device:TPU:0, one launch (start us, length us, event | category | flops | bytes accessed | tf_op | source)
XLA Modules:
  0.0 596.7 jit_solution(1573362764066964522)
XLA Ops:
  11.6 11.2 %all-to-all-start = ((s32[1,1,128,128]{3,1,0,2:T(1,128)}), s32[1,1,128,128]{3,1,0,2:T(1,128)S(1)}, u32[]{:S(2)}, u32[]{:S(2)}) async-start(s32[1,1,128,128]{3,1,0,2:T(1,128)} %bitcast), calls=%async_computation | async-start | bytes 131072 | tf_op jit(solution)/shard_map/all_to_all | solution.py:80
  25.4 6.7 %all-to-all-done = s32[1,1,128,128]{3,1,0,2:T(1,128)S(1)} async-done(((s32[1,1,128,128]{3,1,0,2:T(1,128)}), s32[1,1,128,128]{3,1,0,2:T(1,128)S(1)}, u32[]{:S(2)}, u32[]{:S(2)}) %all-to-all-start) | async-done | bytes 65568 | tf_op jit(solution)/shard_map/all_to_all | solution.py:80
  32.2 4.6 all-to-all-start.1
  37.0 24.4 %all-to-all-done.1 = f32[1,21,128,128]{3,1,0,2:T(8,128)S(1)} async-done(((f32[1,21,128,128]{3,1,0,2:T(8,128)}), f32[1,21,128,128]{3,1,0,2:T(8,128)S(1)}, u32[]{:S(2)}, u32[]{:S(2)}) %all-to-all-start.1) | async-done | bytes 1376288 | tf_op jit(solution)/shard_map/all_to_all | solution.py:79
  62.7 4.7 copy.135
  67.4 90.6 %scatter_custom_fusion = f32[21,12288]{0,1:T(8,128)} fusion(s32[16384]{0:T(1024)S(1)} %bitcast.41, f32[16384,21]{1,0:T(8,128)} %copy.135, f32[]{:T(128)} %constant.109.clone.1), kind=kCustom, calls=%fused_computation.5 | custom fusion | flops 344064 | bytes 1032704 | tf_op jit(solution)/shard_map/scatter-add | solution.py:86
  158.0 4.6 copy.136
  168.1 4.7 collective-permute-start.7
  175.2 6.0 %collective-permute-done.6 = f32[23,48,7]{1,0,2:T(8,128)S(1)} collective-permute-done((f32[23,48,7]{1,0,2:T(8,128)S(1)}, f32[23,48,7]{1,0,2:T(8,128)S(1)}, u32[]{:S(2)}, u32[]{:S(2)}) %collective-permute-start.6) | collective-permute-done | bytes 30944 | tf_op jit(solution)/shard_map/ppermute | solution.py:18
  185.4 3.5 collective-permute-start.8
  189.8 2.0 collective-permute-start
  196.4 13.6 %collective-permute-done.1 = f32[21,48,6]{2,1,0:T(8,128)S(1)} collective-permute-done((f32[21,48,6]{2,1,0:T(8,128)}, f32[21,48,6]{2,1,0:T(8,128)S(1)}, u32[]{:S(2)}, u32[]{:S(2)}) %collective-permute-start.1) | collective-permute-done | bytes 24224 | tf_op jit(solution)/shard_map/ppermute | solution.py:21
  210.0 3.0 collective-permute-done
  215.3 3.7 collective-permute-start.2
  220.1 2.4 copy.143
  223.5 3.4 pad_maximum_fusion.1
  226.9 9.8 %copy.154 = f32[23,7,4096]{0,1,2:T(8,128)} copy(f32[23,7,4096]{2,0,1:T(8,128)} %all-gather.6.cloned.1.call-done) | data formatting | bytes 5275648 | tf_op jit(solution)/shard_map/all_gather | solution.py:30
  236.7 7.5 %gather_fusion = f32[270,23,7]{1,2,0:T(8,128)} fusion(f32[23,7,4096]{0,1,2:T(8,128)} %copy.154, s32[1024]{0:T(1024)S(1)} %copy-done.28), kind=kCustom, calls=%fused_computation.2 | custom fusion | bytes 348840 | tf_op jit(solution)/shard_map/jit(_take)/gather | solution.py:31
  250.3 3.6 scatter.11
  255.3 10.1 %add_add_fusion = (f32[21,60,268]{2,1,0:T(8,128)S(1)}, f32[21,60,268]{2,1,0:T(8,128)}, f32[21,60,268]{2,1,0:T(8,128)}, f32[21,60,268]{2,1,0:T(8,128)}, f32[21,60,268]{2,1,0:T(8,128)}) fusion(f32[23,62,270]{2,1,0:T(8,128)} %copy-done.8, f32[60,268]{1,0:T(8,128)S(1)} %get-tuple-element.59, f32[21]{0:T(128)S(1)} %copy-done.35, ...), kind=kLoop, calls=%fused_computation.32 | loop fusion | flops 5402880 | bytes 13764564 | tf_op jit(solution)/shard_map/add | solution.py:48
  265.4 9.7 %copy.142 = f32[21,6,4096]{0,1,2:T(8,128)} copy(f32[21,6,4096]{2,0,1:T(8,128)} %all-gather.4.cloned.1.call-done) | data formatting | bytes 4128768 | tf_op jit(solution)/shard_map/all_gather | solution.py:30
  275.1 7.5 %gather_fusion.2 = f32[268,21,6]{1,2,0:T(8,128)} fusion(f32[21,6,4096]{0,1,2:T(8,128)} %copy.142, s32[1024]{0:T(1024)S(1)} %pad_clamp_fusion.1), kind=kCustom, calls=%fused_computation.clone | custom fusion | bytes 271216 | tf_op jit(solution)/shard_map/jit(_take)/gather | solution.py:31
  287.9 2.0 scatter.10
  289.9 13.8 %fusion.8 = f32[21,58,266]{2,1,0:T(8,128)} fusion(f32[21,60,268]{2,1,0:T(8,128)} %scatter.10, f32[21,60,268]{2,1,0:T(8,128)S(1)} %get-tuple-element.51, f32[21,60,268]{2,1,0:T(8,128)} %get-tuple-element.55, f32[21,60,268]{2,1,0:T(8,128)} %get-tuple-element.54, f32[21,60,268]{2,1,0:T(8,128)} %get-tuple-element.53, f32[21,60,268]{2,1,0:T(8,128)} %get-tuple-element.52), kind=kLoop, calls=%fused_computation.19 | loop fusion | flops 2915892 | bytes 14255472 | tf_op jit(solution)/shard_map/div | solution.py:101
  303.8 10.9 %fusion.48 = f32[21,56,264]{2,1,0:T(8,128)} fusion(f32[21,58,266]{2,1,0:T(8,128)} %fusion.8, f32[21,60,268]{2,1,0:T(8,128)} %scatter.10, f32[21,60,268]{2,1,0:T(8,128)S(1)} %get-tuple-element.51, f32[21,60,268]{2,1,0:T(8,128)} %get-tuple-element.55, f32[21,60,268]{2,1,0:T(8,128)S(1)} %copy-done.4, f32[21,60,268]{2,1,0:T(8,128)S(1)} %copy-done.2, ...), kind=kLoop, calls=%fused_computation.101 | loop fusion | flops 2794176 | bytes 13660416 | tf_op jit(solution)/shard_map/div | solution.py:101
  314.7 11.0 %fusion.43 = f32[21,54,262]{2,1,0:T(8,128)} fusion(f32[21,56,264]{2,1,0:T(8,128)} %fusion.48, f32[21,60,268]{2,1,0:T(8,128)} %scatter.10, f32[21,60,268]{2,1,0:T(8,128)S(1)} %get-tuple-element.51, f32[21,60,268]{2,1,0:T(8,128)} %get-tuple-element.55, f32[21,60,268]{2,1,0:T(8,128)S(1)} %copy-done.4, f32[21,60,268]{2,1,0:T(8,128)S(1)} %copy-done.2, ...), kind=kLoop, calls=%fused_computation.92 | loop fusion | flops 2673972 | bytes 13072752 | tf_op jit(solution)/shard_map/div | solution.py:101
  325.7 10.2 %fusion.38 = f32[21,52,260]{2,1,0:T(8,128)} fusion(f32[21,54,262]{2,1,0:T(8,128)} %fusion.43, f32[21,60,268]{2,1,0:T(8,128)} %scatter.10, f32[21,60,268]{2,1,0:T(8,128)S(1)} %get-tuple-element.51, f32[21,60,268]{2,1,0:T(8,128)S(1)} %copy-done.6, f32[21,60,268]{2,1,0:T(8,128)S(1)} %copy-done.4, f32[21,60,268]{2,1,0:T(8,128)S(1)} %copy-done.2, ...), kind=kLoop, calls=%fused_computation.83 | loop fusion | flops 2555280 | bytes 12492480 | tf_op jit(solution)/shard_map/div | solution.py:101
  335.9 10.6 %fusion.33 = f32[21,50,258]{2,1,0:T(8,128)} fusion(f32[21,52,260]{2,1,0:T(8,128)} %fusion.38, f32[21,60,268]{2,1,0:T(8,128)} %scatter.10, f32[21,60,268]{2,1,0:T(8,128)S(1)} %get-tuple-element.51, f32[21,60,268]{2,1,0:T(8,128)S(1)} %copy-done.6, f32[21,60,268]{2,1,0:T(8,128)S(1)} %copy-done.4, f32[21,60,268]{2,1,0:T(8,128)S(1)} %copy-done.2, ...), kind=kLoop, calls=%fused_computation.74 | loop fusion | flops 2438100 | bytes 11919600 | tf_op jit(solution)/shard_map/div | solution.py:101
  346.6 6.5 %fusion.60 = f32[21,48,256]{2,1,0:T(8,128)S(1)} fusion(f32[21,50,258]{2,1,0:T(8,128)} %fusion.33, f32[21,60,268]{2,1,0:T(8,128)} %scatter.10, f32[21,60,268]{2,1,0:T(8,128)S(1)} %get-tuple-element.51, f32[21,60,268]{2,1,0:T(8,128)S(1)} %copy-done.6, f32[21,60,268]{2,1,0:T(8,128)S(1)} %copy-done.4, f32[21,60,268]{2,1,0:T(8,128)S(1)} %copy-done.2, ...), kind=kLoop, calls=%fused_computation.131 | loop fusion | flops 2322432 | bytes 11354112 | tf_op jit(solution)/shard_map/div | solution.py:101
  356.1 11.8 %collective-permute-done.11 = f32[21,48,6]{2,1,0:T(8,128)S(1)} collective-permute-done((f32[21,48,6]{2,1,0:T(8,128)S(1)}, f32[21,48,6]{2,1,0:T(8,128)S(1)}, u32[]{:S(2)}, u32[]{:S(2)}) %collective-permute-start.11) | collective-permute-done | bytes 24224 | tf_op jit(solution)/shard_map/ppermute | solution.py:21
  367.9 5.1 collective-permute-done.10
  375.3 3.7 collective-permute-start.12
  379.8 2.4 copy.163
  383.2 3.3 pad_maximum_fusion.2
  386.5 15.0 %all-gather.8.cloned.1.call-done = f32[21,6,4096]{2,0,1:T(8,128)} async-done(((f32[21,6,256]{2,0,1:T(8,128)}), f32[21,6,4096]{2,0,1:T(8,128)}) %all-gather.8.cloned.1.call-update) | async-done | bytes 2064400 | tf_op jit(solution)/shard_map/all_gather | solution.py:30
  401.5 9.7 %copy.162 = f32[21,6,4096]{0,1,2:T(8,128)} copy(f32[21,6,4096]{2,0,1:T(8,128)} %all-gather.8.cloned.1.call-done) | data formatting | bytes 4128768 | tf_op jit(solution)/shard_map/all_gather | solution.py:30
  411.2 7.5 %gather_fusion.3 = f32[268,21,6]{1,2,0:T(8,128)} fusion(f32[21,6,4096]{0,1,2:T(8,128)} %copy.162, s32[1024]{0:T(1024)S(1)} %pad_clamp_fusion.1), kind=kCustom, calls=%fused_computation.1.clone | custom fusion | bytes 271216 | tf_op jit(solution)/shard_map/jit(_take)/gather | solution.py:31
  424.0 2.0 scatter.14
  426.0 13.6 %fusion.3 = f32[21,58,266]{2,1,0:T(8,128)} fusion(f32[21,60,268]{2,1,0:T(8,128)} %scatter.14, f32[21,60,268]{2,1,0:T(8,128)S(1)} %get-tuple-element.51, f32[21,60,268]{2,1,0:T(8,128)} %get-tuple-element.55, f32[21,60,268]{2,1,0:T(8,128)} %get-tuple-element.54, f32[21,60,268]{2,1,0:T(8,128)} %get-tuple-element.53, f32[21,60,268]{2,1,0:T(8,128)} %get-tuple-element.52), kind=kLoop, calls=%fused_computation.10 | loop fusion | flops 2915892 | bytes 14255472 | tf_op jit(solution)/shard_map/div | solution.py:101
  439.6 11.2 %fusion.28 = f32[21,56,264]{2,1,0:T(8,128)} fusion(f32[21,58,266]{2,1,0:T(8,128)} %fusion.3, f32[21,60,268]{2,1,0:T(8,128)} %scatter.14, f32[21,60,268]{2,1,0:T(8,128)S(1)} %get-tuple-element.51, f32[21,60,268]{2,1,0:T(8,128)} %get-tuple-element.55, f32[21,60,268]{2,1,0:T(8,128)S(1)} %copy-done.5, f32[21,60,268]{2,1,0:T(8,128)S(1)} %copy-done.3, ...), kind=kLoop, calls=%fused_computation.65 | loop fusion | flops 2794176 | bytes 13660416 | tf_op jit(solution)/shard_map/div | solution.py:101
  450.8 11.1 %fusion.23 = f32[21,54,262]{2,1,0:T(8,128)} fusion(f32[21,56,264]{2,1,0:T(8,128)} %fusion.28, f32[21,60,268]{2,1,0:T(8,128)} %scatter.14, f32[21,60,268]{2,1,0:T(8,128)S(1)} %get-tuple-element.51, f32[21,60,268]{2,1,0:T(8,128)} %get-tuple-element.55, f32[21,60,268]{2,1,0:T(8,128)S(1)} %copy-done.5, f32[21,60,268]{2,1,0:T(8,128)S(1)} %copy-done.3, ...), kind=kLoop, calls=%fused_computation.56 | loop fusion | flops 2673972 | bytes 13072752 | tf_op jit(solution)/shard_map/div | solution.py:101
  461.9 10.2 %fusion.18 = f32[21,52,260]{2,1,0:T(8,128)} fusion(f32[21,54,262]{2,1,0:T(8,128)} %fusion.23, f32[21,60,268]{2,1,0:T(8,128)} %scatter.14, f32[21,60,268]{2,1,0:T(8,128)S(1)} %get-tuple-element.51, f32[21,60,268]{2,1,0:T(8,128)S(1)} %copy-done.7, f32[21,60,268]{2,1,0:T(8,128)S(1)} %copy-done.5, f32[21,60,268]{2,1,0:T(8,128)S(1)} %copy-done.3, ...), kind=kLoop, calls=%fused_computation.47 | loop fusion | flops 2555280 | bytes 12492480 | tf_op jit(solution)/shard_map/div | solution.py:101
  472.1 10.4 %fusion.13 = f32[21,50,258]{2,1,0:T(8,128)} fusion(f32[21,52,260]{2,1,0:T(8,128)} %fusion.18, f32[21,60,268]{2,1,0:T(8,128)} %scatter.14, f32[21,60,268]{2,1,0:T(8,128)S(1)} %get-tuple-element.51, f32[21,60,268]{2,1,0:T(8,128)S(1)} %copy-done.7, f32[21,60,268]{2,1,0:T(8,128)S(1)} %copy-done.5, f32[21,60,268]{2,1,0:T(8,128)S(1)} %copy-done.3, ...), kind=kLoop, calls=%fused_computation.38 | loop fusion | flops 2438100 | bytes 11919600 | tf_op jit(solution)/shard_map/div | solution.py:101
  482.5 6.7 %fusion.55 = f32[21,48,256]{2,1,0:T(8,128)S(1)} fusion(f32[21,50,258]{2,1,0:T(8,128)} %fusion.13, f32[21,60,268]{2,1,0:T(8,128)} %scatter.14, f32[21,60,268]{2,1,0:T(8,128)S(1)} %get-tuple-element.51, f32[21,60,268]{2,1,0:T(8,128)S(1)} %copy-done.7, f32[21,60,268]{2,1,0:T(8,128)S(1)} %copy-done.5, f32[21,60,268]{2,1,0:T(8,128)S(1)} %copy-done.3, ...), kind=kLoop, calls=%fused_computation.122 | loop fusion | flops 2580480 | bytes 11354196 | tf_op jit(solution)/shard_map/mul | solution.py:109
  489.2 4.0 copy.168
  493.2 57.6 %gather_fusion.1 = f32[16384,21]{1,0:T(8,128)} fusion(f32[21,12288]{0,1:T(8,128)} %bitcast.35, s32[16384]{0:T(1024)S(1)} %broadcast_clamp_fusion), kind=kCustom, calls=%fused_computation.3 | custom fusion | bytes 2818048 | tf_op jit(solution)/shard_map/gather | solution.py:110
  550.8 5.2 copy.166
  556.0 32.2 %all_to_all.15 = f32[1,21,128,128]{3,1,0,2:T(8,128)S(1)} all-to-all(f32[1,21,128,128]{3,1,0,2:T(8,128)S(1)} %copy.166), channel_id=1, replica_groups=mesh['lat'=8,'lon'=16] {'lat','lon'}, dimensions={2} | all-to-all | bytes 2752512 | tf_op jit(solution)/shard_map/all_to_all | solution.py:111
  (161 shorter events, 56.7 us)
Async XLA Ops:
  7.2 219.8 %all-gather.6.cloned.1.call-start = ((), (), s32[]{:S(2)}) async-start(), calls=%async_computation.4 | async-start | bytes 2924544 | tf_op jit(solution)/shard_map/all_gather | solution.py:30
  9.1 13.6 %copy-start.34 = (s32[1,128]{1,0:T(1,128)S(1)}, s32[1,128]{1,0:T(1,128)}, u32[]{:S(2)}) copy-start(s32[1,128]{1,0:T(1,128)} %param.18) | copy-start | bytes 1540
  9.1 14.3 %copy-start.17 = (f32[1,21,128,128]{3,2,1,0:T(8,128)S(1)}, f32[1,21,128,128]{3,2,1,0:T(8,128)}, u32[]{:S(2)}) copy-start(f32[1,21,128,128]{3,2,1,0:T(8,128)} %param.16) | copy-start | bytes 4128772
  11.6 20.6 %all-to-all-start = ((s32[1,1,128,128]{3,1,0,2:T(1,128)}), s32[1,1,128,128]{3,1,0,2:T(1,128)S(1)}, u32[]{:S(2)}, u32[]{:S(2)}) async-start(s32[1,1,128,128]{3,1,0,2:T(1,128)} %bitcast), calls=%async_computation | async-start | bytes 131072 | tf_op jit(solution)/shard_map/all_to_all | solution.py:80
  32.2 29.2 %all-to-all-start.1 = ((f32[1,21,128,128]{3,1,0,2:T(8,128)}), f32[1,21,128,128]{3,1,0,2:T(8,128)S(1)}, u32[]{:S(2)}, u32[]{:S(2)}) async-start(f32[1,21,128,128]{3,1,0,2:T(8,128)} %copy_multiply_fusion), calls=%async_computation.1 | async-start | bytes 3145728 | tf_op jit(solution)/shard_map/all_to_all | solution.py:79
  36.8 228.6 %all-gather.4.cloned.1.call-start = ((), (), s32[]{:S(2)}) async-start(), calls=%async_computation.3 | async-start | bytes 2506752 | tf_op jit(solution)/shard_map/all_gather | solution.py:30
  36.9 30.5 %copy-start.24 = (s32[16384,1]{0,1:T(1,128)}, s32[16384,1]{0,1:T(1,128)S(1)}, u32[]{:S(2)}) copy-start(s32[16384,1]{0,1:T(1,128)S(1)} %compare_select_fusion.1) | copy-start | bytes 196612
  158.0 4.6 copy-start.26
  158.0 4.6 copy-start.31
  158.0 4.6 copy-start.33
  162.6 3.1 copy-start.23
  163.6 237.9 %all-gather.8.cloned.1.call-start = ((), (), s32[]{:S(2)}) async-start(), calls=%async_computation.5 | async-start | bytes 2506752 | tf_op jit(solution)/shard_map/all_gather | solution.py:30
  163.7 9.5 %collective-permute-start.5 = (s32[7]{0:T(128)S(1)}, s32[7]{0:T(128)S(1)}, u32[]{:S(2)}, u32[]{:S(2)}) collective-permute-start(s32[7]{0:T(128)S(1)} %get-tuple-element.73), channel_id=1, source_target_pairs={{1,0},{2,1},{3,2},{4,3},{5,4},{6,5},{7,6},{8,7},{9,8},{10,9},{11,1... | collective-permute-start | bytes 92 | tf_op jit(solution)/shard_map/ppermute | solution.py:21
  165.0 8.1 %collective-permute-start.4 = (s32[7]{0:T(128)S(1)}, s32[7]{0:T(128)S(1)}, u32[]{:S(2)}, u32[]{:S(2)}) collective-permute-start(s32[7]{0:T(128)S(1)} %get-tuple-element.72), channel_id=1, source_target_pairs={{0,1},{1,2},{2,3},{3,4},{4,5},{5,6},{6,7},{7,8},{8,9},{9,10},{10,1... | collective-permute-start | bytes 92 | tf_op jit(solution)/shard_map/ppermute | solution.py:18
  166.7 15.6 %copy-start.11 = (f32[23,48,256]{2,0,1:T(8,128)S(1)}, f32[23,48,256]{2,0,1:T(8,128)}, u32[]{:S(2)}) copy-start(f32[23,48,256]{2,0,1:T(8,128)} %copy-done.10) | copy-start | bytes 3391492
  168.1 6.8 %collective-permute-start.7 = (f32[23,48,7]{1,0,2:T(8,128)S(1)}, f32[23,48,7]{1,0,2:T(8,128)S(1)}, u32[]{:S(2)}, u32[]{:S(2)}) collective-permute-start(f32[23,48,7]{1,0,2:T(8,128)S(1)} %copy.172), channel_id=1, source_target_pairs={{1,0},{2,1},{3,2},{4,3},{5,4},{6,5},{7,6},{8,7},{9,8},{10,9},{11,1... | collective-permute-start | bytes 92744 | tf_op jit(solution)/shard_map/ppermute | solution.py:21
  173.1 8.1 %collective-permute-start.6 = (f32[23,48,7]{1,0,2:T(8,128)S(1)}, f32[23,48,7]{1,0,2:T(8,128)S(1)}, u32[]{:S(2)}, u32[]{:S(2)}) collective-permute-start(f32[23,48,7]{1,0,2:T(8,128)S(1)} %copy.171), channel_id=1, source_target_pairs={{0,1},{1,2},{2,3},{3,4},{4,5},{5,6},{6,7},{7,8},{8,9},{9,10},{10,1... | collective-permute-start | bytes 92744 | tf_op jit(solution)/shard_map/ppermute | solution.py:18
  184.1 10.0 %collective-permute-start.9 = (f32[23,7,270]{2,0,1:T(8,128)S(1)}, f32[23,7,270]{2,0,1:T(8,128)S(1)}, u32[]{:S(2)}, u32[]{:S(2)}) collective-permute-start(f32[23,7,270]{2,0,1:T(8,128)S(1)} %get-tuple-element.65), channel_id=1, source_target_pairs={{16,0},{32,16},{48,32},{64,48},{80,64},{96,80},{112,96},{17,1},{33... | collective-permute-start | bytes 521648 | tf_op jit(solution)/shard_map/ppermute | solution.py:21
  185.4 11.0 %collective-permute-start.8 = (f32[23,7,270]{2,0,1:T(8,128)S(1)}, f32[23,7,270]{2,0,1:T(8,128)S(1)}, u32[]{:S(2)}, u32[]{:S(2)}) collective-permute-start(f32[23,7,270]{2,0,1:T(8,128)S(1)} %get-tuple-element.64), channel_id=1, source_target_pairs={{0,16},{16,32},{32,48},{48,64},{64,80},{80,96},{96,112},{1,17},{17... | collective-permute-start | bytes 521648 | tf_op jit(solution)/shard_map/ppermute | solution.py:18
  189.8 20.2 %collective-permute-start.1 = (f32[21,48,6]{2,1,0:T(8,128)}, f32[21,48,6]{2,1,0:T(8,128)S(1)}, u32[]{:S(2)}, u32[]{:S(2)}) collective-permute-start(f32[21,48,6]{2,1,0:T(8,128)} %get-tuple-element.71), channel_id=1, source_target_pairs={{1,0},{2,1},{3,2},{4,3},{5,4},{6,5},{7,6},{8,7},{9,8},{10,9},{11,1... | collective-permute-start | bytes 72584 | tf_op jit(solution)/shard_map/ppermute | solution.py:21
  189.8 23.2 %collective-permute-start = (f32[21,48,6]{2,1,0:T(8,128)S(1)}, f32[21,48,6]{2,1,0:T(8,128)S(1)}, u32[]{:S(2)}, u32[]{:S(2)}) collective-permute-start(f32[21,48,6]{2,1,0:T(8,128)S(1)} %get-tuple-element.70), channel_id=1, source_target_pairs={{0,1},{1,2},{2,3},{3,4},{4,5},{5,6},{6,7},{7,8},{8,9},{9,10},{10,1... | collective-permute-start | bytes 72584 | tf_op jit(solution)/shard_map/ppermute | solution.py:18
  196.4 22.6 %copy-start.9 = (f32[23,48,270]{2,1,0:T(8,128)S(1)}, f32[23,48,270]{2,1,0:T(8,128)}, u32[]{:S(2)}) copy-start(f32[23,48,270]{2,1,0:T(8,128)} %copy.151) | copy-start | bytes 3576964
  196.4 22.6 %copy-start.18 = (f32[23,7,270]{2,1,0:T(8,128)S(1)}, f32[23,7,270]{2,1,0:T(8,128)}, u32[]{:S(2)}) copy-start(f32[23,7,270]{2,1,0:T(8,128)} %copy.152) | copy-start | bytes 521644
  210.0 5.3 copy-start.13
  213.3 6.1 %collective-permute-start.3 = (f32[21,6,268]{2,0,1:T(8,128)S(1)}, f32[21,6,268]{2,0,1:T(8,128)S(1)}, u32[]{:S(2)}, u32[]{:S(2)}) collective-permute-start(f32[21,6,268]{2,0,1:T(8,128)S(1)} %copy.170), channel_id=1, source_target_pairs={{16,0},{32,16},{48,32},{64,48},{80,64},{96,80},{112,96},{17,1},{33... | collective-permute-start | bytes 405224 | tf_op jit(solution)/shard_map/ppermute | solution.py:21
  215.3 7.2 %collective-permute-start.2 = (f32[21,6,268]{2,0,1:T(8,128)}, f32[21,6,268]{2,0,1:T(8,128)}, u32[]{:S(2)}, u32[]{:S(2)}) collective-permute-start(f32[21,6,268]{2,0,1:T(8,128)} %copy.169), channel_id=1, source_target_pairs={{0,16},{16,32},{32,48},{48,64},{64,80},{80,96},{96,112},{1,17},{17... | collective-permute-start | bytes 405224 | tf_op jit(solution)/shard_map/ppermute | solution.py:18
  226.9 9.8 %copy-start.28 = (s32[1024]{0:T(1024)S(1)}, s32[1024]{0:T(1024)}, u32[]{:S(2)}) copy-start(s32[1024]{0:T(1024)} %pad_clamp_fusion) | copy-start | bytes 12292
  226.9 17.3 %copy-start.30 = (pred[270]{0:T(512)(128)(4,1)S(1)}, pred[270]{0:T(512)(128)(4,1)}, u32[]{:S(2)}) copy-start(pred[270]{0:T(512)(128)(4,1)} %compare_and_fusion.1) | copy-start | bytes 814
  249.0 6.3 %copy-start.35 = (f32[21]{0:T(128)S(1)}, f32[21]{0:T(128)}, u32[]{:S(2)}) copy-start(f32[21]{0:T(128)} %param.22) | copy-start | bytes 256
  265.4 17.2 %copy-start.29 = (pred[268]{0:T(512)(128)(4,1)S(1)}, pred[268]{0:T(512)(128)(4,1)}, u32[]{:S(2)}) copy-start(pred[268]{0:T(512)(128)(4,1)} %compare_and_fusion) | copy-start | bytes 808
  289.9 13.9 %copy-start = (f32[21,60,268]{2,1,0:T(8,128)S(1)}, f32[21,60,268]{2,1,0:T(8,128)}, u32[]{:S(2)}) copy-start(f32[21,60,268]{2,1,0:T(8,128)} %get-tuple-element.52) | copy-start | bytes 4052164
  289.9 13.8 %copy-start.2 = (f32[21,60,268]{2,1,0:T(8,128)S(1)}, f32[21,60,268]{2,1,0:T(8,128)}, u32[]{:S(2)}) copy-start(f32[21,60,268]{2,1,0:T(8,128)} %get-tuple-element.53) | copy-start | bytes 4052164
  289.9 13.8 %copy-start.4 = (f32[21,60,268]{2,1,0:T(8,128)S(1)}, f32[21,60,268]{2,1,0:T(8,128)}, u32[]{:S(2)}) copy-start(f32[21,60,268]{2,1,0:T(8,128)} %get-tuple-element.54) | copy-start | bytes 4052164
  314.7 11.0 %copy-start.6 = (f32[21,60,268]{2,1,0:T(8,128)S(1)}, f32[21,60,268]{2,1,0:T(8,128)}, u32[]{:S(2)}) copy-start(f32[21,60,268]{2,1,0:T(8,128)} %get-tuple-element.55) | copy-start | bytes 4052164
  354.0 25.0 %copy-start.25 = (s32[16384,1]{0,1:T(1,128)S(1)}, s32[16384,1]{0,1:T(1,128)}, u32[]{:S(2)}) copy-start(s32[16384,1]{0,1:T(1,128)} %copy-done.24) | copy-start | bytes 196612
  354.0 13.9 %collective-permute-start.11 = (f32[21,48,6]{2,1,0:T(8,128)S(1)}, f32[21,48,6]{2,1,0:T(8,128)S(1)}, u32[]{:S(2)}, u32[]{:S(2)}) collective-permute-start(f32[21,48,6]{2,1,0:T(8,128)S(1)} %get-tuple-element.69), channel_id=1, source_target_pairs={{1,0},{2,1},{3,2},{4,3},{5,4},{6,5},{7,6},{8,7},{9,8},{10,9},{11,1... | collective-permute-start | bytes 72584 | tf_op jit(solution)/shard_map/ppermute | solution.py:21
  354.5 18.4 %collective-permute-start.10 = (f32[21,48,6]{2,1,0:T(8,128)S(1)}, f32[21,48,6]{2,1,0:T(8,128)S(1)}, u32[]{:S(2)}, u32[]{:S(2)}) collective-permute-start(f32[21,48,6]{2,1,0:T(8,128)S(1)} %get-tuple-element.68), channel_id=1, source_target_pairs={{0,1},{1,2},{2,3},{3,4},{4,5},{5,6},{6,7},{7,8},{8,9},{9,10},{10,1... | collective-permute-start | bytes 72584 | tf_op jit(solution)/shard_map/ppermute | solution.py:18
  367.9 11.1 %copy-start.15 = (f32[21,48,6]{2,1,0:T(8,128)}, f32[21,48,6]{2,1,0:T(8,128)S(1)}, u32[]{:S(2)}) copy-start(f32[21,48,6]{2,1,0:T(8,128)S(1)} %collective-permute-done.11) | copy-start | bytes 72580
  372.9 6.1 %copy-start.16 = (f32[21,48,6]{2,1,0:T(8,128)}, f32[21,48,6]{2,1,0:T(8,128)S(1)}, u32[]{:S(2)}) copy-start(f32[21,48,6]{2,1,0:T(8,128)S(1)} %collective-permute-done.10) | copy-start | bytes 72580
  373.2 5.8 collective-permute-start.13
  375.3 6.9 %collective-permute-start.12 = (f32[21,6,268]{2,0,1:T(8,128)}, f32[21,6,268]{2,0,1:T(8,128)}, u32[]{:S(2)}, u32[]{:S(2)}) collective-permute-start(f32[21,6,268]{2,0,1:T(8,128)} %copy.173), channel_id=1, source_target_pairs={{0,16},{16,32},{32,48},{48,64},{64,80},{80,96},{96,112},{1,17},{17... | collective-permute-start | bytes 405224 | tf_op jit(solution)/shard_map/ppermute | solution.py:18
  426.0 13.6 %copy-start.1 = (f32[21,60,268]{2,1,0:T(8,128)S(1)}, f32[21,60,268]{2,1,0:T(8,128)}, u32[]{:S(2)}) copy-start(f32[21,60,268]{2,1,0:T(8,128)} %get-tuple-element.52) | copy-start | bytes 4052164
  426.0 13.6 %copy-start.3 = (f32[21,60,268]{2,1,0:T(8,128)S(1)}, f32[21,60,268]{2,1,0:T(8,128)}, u32[]{:S(2)}) copy-start(f32[21,60,268]{2,1,0:T(8,128)} %get-tuple-element.53) | copy-start | bytes 4052164
  426.0 13.6 %copy-start.5 = (f32[21,60,268]{2,1,0:T(8,128)S(1)}, f32[21,60,268]{2,1,0:T(8,128)}, u32[]{:S(2)}) copy-start(f32[21,60,268]{2,1,0:T(8,128)} %get-tuple-element.54) | copy-start | bytes 4052164
  450.8 11.1 %copy-start.7 = (f32[21,60,268]{2,1,0:T(8,128)S(1)}, f32[21,60,268]{2,1,0:T(8,128)}, u32[]{:S(2)}) copy-start(f32[21,60,268]{2,1,0:T(8,128)} %get-tuple-element.55) | copy-start | bytes 4052164
  472.1 10.4 %copy-start.32 = (f32[21]{0:T(128)S(1)}, f32[21]{0:T(128)}, u32[]{:S(2)}) copy-start(f32[21]{0:T(128)} %param.23) | copy-start | bytes 256
  489.2 4.0 copy-start.12
  556.0 32.2 %copy-start.22 = (f32[128,128]{1,0:T(8,128)S(1)}, f32[128,128]{1,0:T(8,128)}, u32[]{:S(2)}) copy-start(f32[128,128]{1,0:T(8,128)} %copy-done.21) | copy-start | bytes 196612
  (7 other events, 7.7 us)
Sparse Core Ops, SparseCore 0:
  11.7 62.4 all-gather.5
  163.7 53.4 all-gather.3
  353.9 47.5 all-gather.7
where the time goes:
time: 606 us; the launch traced here: 597 us
  other arithmetic  253 us (42%)
  local copies, waits for them, and re-layouts  169 us (28%)
  waiting for transfers between devices  85.9 us (14%)
  starting transfers between devices  41.7 us (7%)
  blocking collectives  32.2 us (5%)
  between operations  14.8 us (2%)
    div x11, other arithmetic, per_device(): (trim_margin(source_wide, depth, inner) + trim_margin(w_east, depth, inne...  120 us
    scatter-add x1, other arithmetic, per_device(): jnp.zeros((channels, tile_rows * tile_cols), jnp.float32).at[:, cell_ids]  90.6 us
    gather x1, local copies, waits for them, and re-layouts, per_device(): local_fit = diffused.reshape(channels, -1)[:, cell_ids]  57.6 us
    all_to_all x1, blocking collectives, per_device(): lax.all_to_all(local_fit.reshape(1, channels, devices, slots), ('lat', 'l...  32.2 us
    all_gather x3, local copies, waits for them, and re-layouts, extend_deep(): lax.all_gather(block[:, tile_rows - depth:, :], 'lon', axis=2, tiled=True)  29.2 us
    ppermute x7, waiting for transfers between devices, with_halo(): lax.ppermute(lax.slice_in_dim(block, 0, width, axis=dim), axis, backward)  25.6 us
    all_to_all x1, waiting for transfers between devices, per_device(): lax.all_to_all(outgoing, ('lat', 'lon'), split_axis=2, concat_axis=2, til...  24.4 us
    gather x3, local copies, waits for them, and re-layouts, extend_deep(): ghost = jnp.take(top_rows, partner_wide, axis=2)[:, ::-1, :]  22.6 us
  transfers between devices with their start and end apart: 19, of which 9 were waited for; matrix products, arithmetic and copies ran while one was open for 29% of the time, Pallas kernels for 0%

commit v1 on v0

v1 whole, which is shorter than its diff:
```python
import functools

import jax
import jax.numpy as jnp
from jax import lax
from jax.experimental import pallas as pl
from jax.experimental.pallas import tpu as pltpu
from jax.sharding import PartitionSpec as P

LEV = 10
C = 21
CP = 24
ROWS = 48
COLS = 256
BAND = ROWS // 2
PLACES = 2 * COLS
DEEP = 12
EXT = ROWS + 2 * DEEP
GRP = 16
CEXT = ROWS + 2 * GRP
F32 = jnp.float32
BF16 = jnp.bfloat16
MESH = pl.DeviceIdType.MESH
VMEM_LIMIT = 60 * 2**20


def place_of(linear, n_lon):
    return (linear // n_lon, lax.rem(linear, n_lon))


def split(cell):
    cell = cell.astype(jnp.int32)
    place = cell & (PLACES - 1)
    low = place & 255
    half = place >> 8
    return cell >> 9, [jnp.where(half == h, low, 512).astype(F32) for h in range(2)]


def store_onehot(onehot, halves, lanes):
    one = jnp.ones((16, 128), BF16)
    zero = jnp.zeros((16, 128), BF16)
    steps = lax.broadcasted_iota(jnp.int32, (16, 128), 0).astype(F32).astype(BF16)
    for h in range(2):
        row = jnp.broadcast_to(halves[h], (16, 128)).astype(BF16)
        for t in range(16):
            first = h * 256 + t * 16
            onehot[first : first + 16, lanes] = jnp.where(row == steps + BF16(16 * t), one, zero)


def build_chunk(arrived, chunk, size, lhs, onehot):
    for j in range(size):
        value = arrived[chunk * size + j]
        band, halves = split(value[C : C + 1, :])
        lanes = slice(j * 128, (j + 1) * 128)
        high = value.astype(BF16)
        pieces = jnp.concatenate([value, value - high.astype(F32)], axis=0).astype(BF16)
        band = jnp.broadcast_to(band.astype(F32), (16, 128)).astype(BF16)
        zero = jnp.zeros((2 * CP, 128), BF16)
        for b in range(BAND):
            mask = jnp.concatenate([band == BF16(b)] * 3, axis=0)
            lhs[b * 2 * CP : (b + 1) * 2 * CP, lanes] = jnp.where(mask, pieces, zero)
        store_onehot(onehot, halves, lanes)


def scatter_kernel(
    n, n_lon, size, value_ref, cell_ref, field_ref, slot_ref,
    outgoing, arrived, lhs0, onehot0, lhs1, onehot1, total, local_sem, send_sem, recv_sem,
):
    me = lax.axis_index("lat") * n_lon + lax.axis_index("lon")
    load = pltpu.make_async_copy(value_ref, outgoing.at[0:C], local_sem.at[0])
    load.start()
    barrier = pltpu.get_barrier_semaphore()

    def greet(i, carry):
        pl.semaphore_signal(barrier, inc=1, device_id=place_of(lax.rem(me + i, n), n_lon), device_id_type=MESH)
        return carry

    lax.fori_loop(1, n, greet, 0)
    outgoing[C] = cell_ref[...]
    total[...] = jnp.zeros_like(total)
    load.wait()
    pl.semaphore_wait(barrier, n - 1)

    def send(i, carry):
        owner = lax.rem(me + i, n)
        pltpu.make_async_remote_copy(
            src_ref=outgoing.at[:, owner, :],
            dst_ref=arrived.at[i, 0 : C + 1, :],
            send_sem=send_sem,
            recv_sem=recv_sem.at[i // size],
            device_id=place_of(owner, n_lon),
            device_id_type=MESH,
        ).start()
        return carry

    own = pltpu.make_async_copy(outgoing.at[:, me, :], arrived.at[0, 0 : C + 1, :], local_sem.at[1])
    own.start()
    lax.fori_loop(1, n, send, 0)
    own.wait()

    def arrive(chunk, first):
        window = arrived.at[pl.ds(chunk * size + first, size - first), 0 : C + 1, :]
        pltpu.make_async_copy(window, window, recv_sem.at[chunk]).wait()

    chunks = n // size
    dims = (((1,), (1,)), ((), ()))
    arrive(0, 1)
    build_chunk(arrived, 0, size, lhs0, onehot0)

    def pair(i, carry):
        arrive(2 * i + 1, 0)
        build_chunk(arrived, 2 * i + 1, size, lhs1, onehot1)
        total[...] += lax.dot_general(lhs0[...], onehot0[...], dims, preferred_element_type=F32)
        more = 2 * i + 2

        @pl.when(more < chunks)
        def _():
            arrive(more, 0)

        build_chunk(arrived, jnp.minimum(more, chunks - 1), size, lhs0, onehot0)
        total[...] += lax.dot_general(lhs1[...], onehot1[...], dims, preferred_element_type=F32)
        return carry

    lax.fori_loop(0, chunks // 2, pair, 0)
    for b in range(BAND):
        first = b * 2 * CP
        band = total[first : first + CP, :] + total[first + CP : first + 2 * CP, :]
        for t in range(4):
            field_ref[t % 2, 2 * b + t // 2] = band[:, t * 128 : (t + 1) * 128]
    slot_ref[...] = arrived[:, C, :]
    sent = arrived.at[1:n, 0 : C + 1, :]
    pltpu.make_async_copy(sent, sent, send_sem).wait()


def scatter(n, n_lon, value, cell):
    size = min(8, n // 4)
    vmem = pl.BlockSpec(memory_space=pltpu.VMEM)
    buffers = [
        pltpu.VMEM((BAND * 2 * CP, size * 128), BF16),
        pltpu.VMEM((PLACES, size * 128), BF16),
    ]
    return pl.pallas_call(
        functools.partial(scatter_kernel, n, n_lon, size),
        out_shape=(
            jax.ShapeDtypeStruct((2, ROWS, CP, 128), F32),
            jax.ShapeDtypeStruct((n, 128), F32),
        ),
        in_specs=[pl.BlockSpec(memory_space=pl.ANY), vmem],
        out_specs=(vmem, vmem),
        scratch_shapes=[
            pltpu.VMEM((C + 1, n, 128), F32),
            pltpu.VMEM((n, CP, 128), F32),
            *buffers,
            *buffers,
            pltpu.VMEM((BAND * 2 * CP, PLACES), F32),
            pltpu.SemaphoreType.DMA((2,)),
            pltpu.SemaphoreType.DMA,
            pltpu.SemaphoreType.DMA((n // size,)),
        ],
        compiler_params=pltpu.CompilerParams(
            collective_id=0, has_side_effects=True, vmem_limit_bytes=VMEM_LIMIT
        ),
        name="scatter",
    )(value, cell)


def lanes_of(shape):
    return lax.broadcasted_iota(jnp.int32, shape, len(shape) - 1)


def east_of(tiles):
    turned = [pltpu.roll(x, 127, x.ndim - 1) for x in tiles]
    last = lanes_of(tiles[0].shape) == 127
    return [jnp.where(last, turned[(t + 1) % 3], turned[t]) for t in range(3)]


def west_of(tiles):
    turned = [pltpu.roll(x, 1, x.ndim - 1) for x in tiles]
    first = lanes_of(tiles[0].shape) == 0
    return [jnp.where(first, turned[(t + 2) % 3], turned[t]) for t in range(3)]


def diffuse_kernel(
    n_lat, n_lon, partner_ref, field_ref, coef_ref, scale_ref, sigma_ref, out_ref,
    cur, nxt, rhs, inv, w_e, w_w, w_n, w_s, pack_e, pack_w, edge_e, edge_w,
    coef, coef_e, coef_w, fold, coef_fold, send_sem, recv_sem, fold_send, fold_recv, local_sem,
):
    lat = lax.axis_index("lat")
    lon = lax.axis_index("lon")
    east = lax.rem(lon + 1, n_lon)
    west = lax.rem(lon + n_lon - 1, n_lon)
    has_n = lat < n_lat - 1
    has_s = lat > 0
    top = lat == n_lat - 1
    everywhere = lat >= 0
    north = jnp.minimum(lat + 1, n_lat - 1)
    south = jnp.maximum(lat - 1, 0)
    ways = [
        (everywhere, lat, east, everywhere),
        (everywhere, lat, west, everywhere),
        (has_n, north, lon, has_s),
        (has_s, south, lon, has_n),
        (has_n, north, east, has_s),
        (has_n, north, west, has_s),
        (has_s, south, east, has_n),
        (has_s, south, west, has_n),
    ]
    barrier = pltpu.get_barrier_semaphore()
    for exists, to_lat, to_lon, _ in ways:
        @pl.when(exists)
        def _():
            pl.semaphore_signal(barrier, inc=1, device_id=(to_lat, to_lon), device_id_type=MESH)

    def greet(i, carry):
        pl.semaphore_signal(barrier, inc=1, device_id=(lat, lax.rem(lon + i, n_lon)), device_id_type=MESH)
        return carry

    @pl.when(top)
    def _():
        lax.fori_loop(1, n_lon, greet, 0)

    lane16 = lanes_of((CP, 128)) >> 4
    for i in range(ROWS // 8):
        first = jnp.zeros((CP, 128), F32)
        last = jnp.zeros((CP, 128), F32)
        for j in range(8):
            x = field_ref[0, 8 * i + j]
            y = field_ref[1, 8 * i + j]
            first = jnp.where(lane16 == j, pltpu.roll(x, 16 * j, 1) if j else x, first)
            last = jnp.where(lane16 == j, pltpu.roll(y, 16 * j + 16, 1) if j < 7 else y, last)
        pack_w[i] = first
        pack_e[i] = last

    @pl.when(lat == 0)
    def _():
        cur[0:2, 0:DEEP] = jnp.zeros((2, DEEP, CP, 128), F32)
        edge_e[0:2] = jnp.zeros((2, CP, 128), F32)
        edge_w[0:2] = jnp.zeros((2, CP, 128), F32)
        coef[:, :, 0:GRP, :] = jnp.zeros((2, 3, GRP, 128), F32)
        coef_e[:, 0:GRP, :] = jnp.zeros((3, GRP, 128), F32)
        coef_w[:, 0:GRP, :] = jnp.zeros((3, GRP, 128), F32)

    @pl.when(top)
    def _():
        edge_e[8:10] = jnp.zeros((2, CP, 128), F32)
        edge_w[8:10] = jnp.zeros((2, CP, 128), F32)
        coef_e[:, GRP + ROWS : CEXT, :] = jnp.zeros((3, GRP, 128), F32)
        coef_w[:, GRP + ROWS : CEXT, :] = jnp.zeros((3, GRP, 128), F32)

    for t in range(2):
        cur[t, DEEP : DEEP + ROWS] = field_ref[t]
        coef[t, :, GRP : GRP + ROWS, :] = coef_ref[t]

    greeted = 2 + 3 * has_n.astype(jnp.int32) + 3 * has_s.astype(jnp.int32) + (n_lon - 1) * top.astype(jnp.int32)
    pl.semaphore_wait(barrier, greeted)

    mid_g, low_g, high_g = pl.ds(GRP, ROWS), pl.ds(0, GRP), pl.ds(GRP + ROWS, GRP)
    head, tail = pl.ds(0, GRP), pl.ds(ROWS - GRP, GRP)
    copies = [
        ((pack_e, edge_w.at[pl.ds(2, 6)]), (coef_ref.at[1], coef_w.at[:, mid_g, :])),
        ((pack_w, edge_e.at[pl.ds(2, 6)]), (coef_ref.at[0], coef_e.at[:, mid_g, :])),
        (
            (field_ref.at[:, pl.ds(ROWS - DEEP, DEEP)], cur.at[pl.ds(0, 2), pl.ds(0, DEEP)]),
            (coef_ref.at[:, :, tail, :], coef.at[:, :, low_g, :]),
        ),
        (
            (field_ref.at[:, pl.ds(0, DEEP)], cur.at[pl.ds(0, 2), pl.ds(EXT - DEEP, DEEP)]),
            (coef_ref.at[:, :, head, :], coef.at[:, :, high_g, :]),
        ),
        ((pack_e.at[pl.ds(4, 2)], edge_w.at[pl.ds(0, 2)]), (coef_ref.at[1, :, tail, :], coef_w.at[:, low_g, :])),
        ((pack_w.at[pl.ds(4, 2)], edge_e.at[pl.ds(0, 2)]), (coef_ref.at[0, :, tail, :], coef_e.at[:, low_g, :])),
        ((pack_e.at[pl.ds(0, 2)], edge_w.at[pl.ds(8, 2)]), (coef_ref.at[1, :, head, :], coef_w.at[:, high_g, :])),
        ((pack_w.at[pl.ds(0, 2)], edge_e.at[pl.ds(8, 2)]), (coef_ref.at[0, :, head, :], coef_e.at[:, high_g, :])),
    ]

    def copy_of(w, k):
        source, target = copies[w][k]
        return pltpu.make_async_remote_copy(
            src_ref=source,
            dst_ref=target,
            send_sem=send_sem.at[w, k],
            recv_sem=recv_sem.at[w, k],
            device_id=(ways[w][1], ways[w][2]),
            device_id_type=MESH,
        )

    for w in range(8):
        @pl.when(ways[w][0])
        def _():
            for k in range(2):
                copy_of(w, k).start()

    mine = pl.ds(2 * lon, 2)
    fold_source = field_ref.at[:, pl.ds(ROWS - DEEP, DEEP)]
    coef_source = coef_ref.at[:, :, tail, :]

    def fold_copies(i):
        to = (lat, lax.rem(lon + i, n_lon))
        return [
            pltpu.make_async_remote_copy(
                src_ref=source,
                dst_ref=target.at[mine],
                send_sem=fold_send.at[k, i],
                recv_sem=fold_recv.at[k, i],
                device_id=to,
                device_id_type=MESH,
            )
            for k, (source, target) in enumerate(((fold_source, fold), (coef_source, coef_fold)))
        ]

    def start_fold(i, carry):
        for copy in fold_copies(i):
            copy.start()
        return carry

    def wait_fold(i, carry):
        for copy in fold_copies(i):
            copy.wait()
        return carry

    @pl.when(top)
    def _():
        lax.fori_loop(1, n_lon, start_fold, 0)
        own = [
            pltpu.make_async_copy(fold_source, fold.at[mine], local_sem.at[0]),
            pltpu.make_async_copy(coef_source, coef_fold.at[mine], local_sem.at[1]),
        ]
        for copy in own:
            copy.start()
        for copy in own:
            copy.wait()

    for w in range(8):
        @pl.when(ways[w][0])
        def _():
            for k in range(2):
                copy_of(w, k).wait_send()

        @pl.when(ways[w][3])
        def _():
            for k in range(2):
                copy_of(w, k).wait_recv()

    side = lanes_of((CP, 128)) < 64

    def unpack(i, carry):
        from_e = edge_e[i]
        from_w = edge_w[i]
        for j in range(8):
            x = pltpu.roll(from_e, 128 - 16 * j, 1) if j else from_e
            y = pltpu.roll(from_w, 112 - 16 * j, 1) if j < 7 else from_w
            row = 8 * i + j - (GRP - DEEP)
            nxt[0, row + (GRP - DEEP)] = jnp.where(side, x, y)
        return carry

    lax.fori_loop(0, CEXT // 8, unpack, 0)
    cur[2] = nxt[0, GRP - DEEP : GRP - DEEP + EXT]
    side_c = lanes_of((3, CEXT, 128)) < 64
    coef_e[...] = jnp.where(side_c, coef_e[...], coef_w[...])

    @pl.when(top)
    def _():
        lax.fori_loop(1, n_lon, wait_fold, 0)
        corner = partner_ref[0]
        tile0 = corner // 128
        shift = lax.rem(corner, 128)
        lane = lanes_of((CP, 128))
        index = (shift - lane) & 127
        near = lane <= shift
        places = [lax.rem(tile0 + x - 4 + 2 * n_lon, 2 * n_lon) for x in range(1, 6)]

        def mirrored(load, index, near, side):
            tiles = [jnp.take_along_axis(load(p), index, axis=1) for p in places]
            merged = [jnp.where(near, tiles[x], tiles[x - 1]) for x in range(1, 5)]
            return merged[2], merged[1], jnp.where(side, merged[0], merged[3])

        def ghost(d, carry):
            tiles = mirrored(lambda p: fold[p, DEEP - 1 - d], index, near, side)
            for t in range(3):
                cur[t, EXT - DEEP + d] = tiles[t]
            return carry

        lax.fori_loop(0, DEEP, ghost, 0)
        lane_c = lanes_of((GRP, 128))
        for k in range(3):
            tiles = mirrored(
                lambda p: coef_fold[p, k], (shift - lane_c) & 127, lane_c <= shift, lane_c < 64
            )
            for d in range(GRP):
                for t in range(2):
                    coef[t, k, GRP + ROWS + d : GRP + ROWS + d + 1, :] = tiles[t][GRP - 1 - d : GRP - d]
                coef_e[k, GRP + ROWS + d : GRP + ROWS + d + 1, :] = tiles[2][GRP - 1 - d : GRP - d]

    channel = lax.broadcasted_iota(jnp.int32, (CP, 128), 0)
    level = jnp.where(channel < LEV, channel, jnp.where(channel < 2 * LEV, channel - LEV, 0))
    level = jnp.where(channel < C, level, 2 * LEV).astype(F32)
    scale = jnp.broadcast_to(scale_ref[...], (CP, 128))
    sigma = jnp.broadcast_to(sigma_ref[...], (CP, 128))

    def coef_row(k, row):
        return [
            jnp.broadcast_to(ref[k, pl.ds(row, 1), :], (CP, 128))
            for ref in (coef.at[0], coef.at[1], coef_e)
        ]

    def weigh(r, carry):
        g = r + (GRP - DEEP)
        wet_here = [(level < b).astype(F32) for b in coef_row(0, g)]
        wet_north = [(level < b).astype(F32) for b in coef_row(0, g + 1)]
        wet_south = [(level < b).astype(F32) for b in coef_row(0, g - 1)]
        k0 = coef_row(1, g)
        k1 = coef_row(2, g)
        k1_north = coef_row(2, g + 1)
        k1_south = coef_row(2, g - 1)
        k0_east, k0_west = east_of(k0), west_of(k0)
        wet_east, wet_west = east_of(wet_here), west_of(wet_here)
        for t in range(3):
            here = scale * wet_here[t]
            e = here * (0.5 * (k0[t] + k0_east[t])) * wet_east[t]
            w = here * (0.5 * (k0[t] + k0_west[t])) * wet_west[t]
            m = here * (0.5 * (k1[t] + k1_north[t])) * wet_north[t]
            s = here * (0.5 * (k1[t] + k1_south[t])) * wet_south[t]
            over = 1.0 / (1.0 + e + w + m + s)
            inv[t, r] = over
            w_e[t, r] = e * over
            w_w[t, r] = w * over
            w_n[t, r] = m * over
            w_s[t, r] = s * over
            start = jnp.where(wet_here[t] > 0.0, cur[t, r] * sigma, 0.0)
            cur[t, r] = start
            rhs[t, r] = start * over
        return carry

    lax.fori_loop(0, EXT, weigh, 0)

    def sweep(source, target, r):
        here = [source[t, r] for t in range(3)]
        to_east, to_west = east_of(here), west_of(here)
        for t in range(3):
            target[t, r] = (
                rhs[t, r]
                + w_e[t, r] * to_east[t]
                + w_w[t, r] * to_west[t]
                + w_n[t, r] * source[t, r + 1]
                + w_s[t, r] * source[t, r - 1]
            )

    source, target = cur, nxt
    for s in range(1, DEEP + 1):
        if s == DEEP // 2 + 1:
            def renew(r, carry, source=source):
                for t in range(3):
                    rhs[t, r] = source[t, r] * inv[t, r]
                return carry

            lax.fori_loop(s, EXT - s, renew, 0)

        def rows(r, carry, source=source, target=target):
            sweep(source, target, r)
            return carry

        lax.fori_loop(s, EXT - s, rows, 0, unroll=2)
        source, target = target, source

    def finish(r, carry):
        for t in range(2):
            out_ref[t, r] = source[t, r + DEEP] * sigma
        return carry

    lax.fori_loop(0, ROWS, finish, 0)


def diffuse(n_lat, n_lon, partner, field, coef, scale, sigma):
    vmem = pl.BlockSpec(memory_space=pltpu.VMEM)
    state = pltpu.VMEM((3, EXT, CP, 128), F32)
    state_wide = pltpu.VMEM((3, CEXT, CP, 128), F32)
    return pl.pallas_call(
        functools.partial(diffuse_kernel, n_lat, n_lon),
        out_shape=jax.ShapeDtypeStruct((2, ROWS, CP, 128), F32),
        in_specs=[pl.BlockSpec(memory_space=pltpu.SMEM), vmem, vmem, vmem, vmem],
        out_specs=vmem,
        scratch_shapes=[
            state,
            state_wide,
            state,
            state,
            state,
            state,
            state,
            state,
            pltpu.VMEM((ROWS // 8, CP, 128), F32),
            pltpu.VMEM((ROWS // 8, CP, 128), F32),
            pltpu.VMEM((CEXT // 8, CP, 128), F32),
            pltpu.VMEM((CEXT // 8, CP, 128), F32),
            pltpu.VMEM((2, 3, CEXT, 128), F32),
            pltpu.VMEM((3, CEXT, 128), F32),
            pltpu.VMEM((3, CEXT, 128), F32),
            pltpu.VMEM((2 * n_lon, DEEP, CP, 128), F32),
            pltpu.VMEM((2 * n_lon, 3, GRP, 128), F32),
            pltpu.SemaphoreType.DMA((8, 2)),
            pltpu.SemaphoreType.DMA((8, 2)),
            pltpu.SemaphoreType.DMA((2, n_lon)),
            pltpu.SemaphoreType.DMA((2, n_lon)),
            pltpu.SemaphoreType.DMA((2,)),
        ],
        compiler_params=pltpu.CompilerParams(
            collective_id=1, has_side_effects=True, vmem_limit_bytes=VMEM_LIMIT
        ),
        name="diffuse",
    )(partner, field, coef, scale, sigma)


def gather_kernel(n, n_lon, size, slot_ref, state_ref, out_ref, pieces, onehot, fits, send_sem, recv_sem, local_sem):
    me = lax.axis_index("lat") * n_lon + lax.axis_index("lon")
    barrier = pltpu.get_barrier_semaphore()

    def greet(i, carry):
        pl.semaphore_signal(barrier, inc=1, device_id=place_of(lax.rem(me + i, n), n_lon), device_id_type=MESH)
        return carry

    lax.fori_loop(1, n, greet, 0)
    for b in range(0, BAND, 2):
        for half in range(2):
            for t in range(2):
                rows = jnp.concatenate(
                    [state_ref[t, 2 * b + half], state_ref[t, 2 * b + 2 + half]], axis=0
                )
                high = rows.astype(BF16)
                low = (rows - high.astype(F32)).astype(BF16)
                first = half * COLS + t * 128
                pieces[b * CP : (b + 2) * CP, first : first + 128] = high
                pieces[b * CP : (b + 2) * CP, PLACES + first : PLACES + first + 128] = low
    pl.semaphore_wait(barrier, n - 1)

    def chunk(g, carry):
        for j in range(size):
            band, halves = split(slot_ref[pl.ds(g * size + j, 1), :])
            store_onehot(onehot, halves, slice(j * 128, (j + 1) * 128))
        picked = jnp.dot(pieces[:, :PLACES], onehot[...], preferred_element_type=F32) + jnp.dot(
            pieces[:, PLACES:], onehot[...], preferred_element_type=F32
        )
        for j in range(size):
            band, halves = split(slot_ref[pl.ds(g * size + j, 1), :])
            band = jnp.broadcast_to(band, (CP, 128))
            fit = jnp.zeros((CP, 128), F32)
            for b in range(BAND):
                fit += jnp.where(band == b, picked[b * CP : (b + 1) * CP, j * 128 : (j + 1) * 128], 0.0)
            fits[g * size + j] = fit
        for j in range(size):
            i = g * size + j
            to = lax.rem(me - i + n, n)

            @pl.when(i > 0)
            def _():
                pltpu.make_async_remote_copy(
                    src_ref=fits.at[i, 0:C, :],
                    dst_ref=out_ref.at[:, me, :],
                    send_sem=send_sem,
                    recv_sem=recv_sem,
                    device_id=place_of(to, n_lon),
                    device_id_type=MESH,
                ).start()

            @pl.when(i == 0)
            def _():
                pltpu.make_async_copy(fits.at[0, 0:C, :], out_ref.at[:, me, :], local_sem).start()

        return carry

    lax.fori_loop(0, n // size, chunk, 0)
    pltpu.make_async_copy(fits.at[0, 0:C, :], out_ref.at[:, me, :], local_sem).wait()
    sent = fits.at[1:n, 0:C, :]
    pltpu.make_async_copy(sent, sent, send_sem).wait()
    pltpu.make_async_copy(sent, sent, recv_sem).wait()


def gather(n, n_lon, slot, state):
    size = min(4, n // 4)
    vmem = pl.BlockSpec(memory_space=pltpu.VMEM)
    return pl.pallas_call(
        functools.partial(gather_kernel, n, n_lon, size),
        out_shape=jax.ShapeDtypeStruct((C, n, 128), F32),
        in_specs=[vmem, vmem],
        out_specs=vmem,
        scratch_shapes=[
            pltpu.VMEM((BAND * CP, 2 * PLACES), BF16),
            pltpu.VMEM((PLACES, size * 128), BF16),
            pltpu.VMEM((n, CP, 128), F32),
            pltpu.SemaphoreType.DMA,
            pltpu.SemaphoreType.DMA,
            pltpu.SemaphoreType.DMA,
        ],
        compiler_params=pltpu.CompilerParams(
            collective_id=2, has_side_effects=True, vmem_limit_bytes=VMEM_LIMIT
        ),
        name="gather",
    )(slot, state)


def per_device(
    n_lat, n_lon, obs_value, obs_cell, obs_count, bottom_level, diffusivity, partner, length_scale, sigma
):
    n = n_lat * n_lon
    slots = lax.broadcasted_iota(jnp.int32, (n, 128), 1)
    cell = jnp.where(slots < obs_count[0][:, None], obs_cell[0], -1).astype(F32)
    coef = jnp.concatenate([bottom_level.astype(F32)[None], diffusivity], axis=0)
    coef = coef.reshape(3, ROWS, 2, 128).transpose(2, 0, 1, 3)
    column = lambda x: jnp.pad(x, (0, CP - C))[:, None]
    field, slot = scatter(n, n_lon, obs_value[0], cell)
    state = diffuse(n_lat, n_lon, partner, field, coef, column(length_scale), column(sigma))
    fit = gather(n, n_lon, slot, state)
    diffused = state[:, :, :C, :].transpose(2, 1, 0, 3).reshape(C, ROWS, COLS)
    return fit[None], diffused


def solution(mesh):
    n_lat, n_lon = mesh.shape["lat"], mesh.shape["lon"]
    return jax.shard_map(
        functools.partial(per_device, n_lat, n_lon),
        mesh=mesh,
        in_specs=(
            P(("lat", "lon"), None, None, None),
            P(("lat", "lon"), None, None),
            P(("lat", "lon"), None),
            P("lat", "lon"),
            P(None, "lat", "lon"),
            P("lon"),
            P(),
            P(),
        ),
        out_specs=(P(("lat", "lon"), None, None, None), P(None, "lat", "lon")),
        check_vma=False,
    )
```

time: 606 us -> 227 us (0.37); the launches traced: 597 us -> 227 us
  other arithmetic: 253 us -> 3.03 us
  Pallas kernels: 0 us -> 214 us
  local copies, waits for them, and re-layouts: 169 us -> 9.25 us
  waiting for transfers between devices: 85.9 us -> 0 us
  starting transfers between devices: 41.7 us -> 0 us
  blocking collectives: 32.2 us -> 0 us
  between operations: 14.8 us -> 0.69 us
    pallas_call x0 -> x3, Pallas kernels: none -> 214 us  [the longest x1 90.3 us: gather(): pl.pallas_call(functools.partial(gather_kernel, n, n_lon, size), out_shap...]
    div x11 -> x0, other arithmetic: 120 us -> none  [per_device(): (trim_margin(source_wide, depth, inner) + trim_margin(w_east, depth, inne...]
    scatter-add x1 -> x0, other arithmetic: 90.6 us -> none  [per_device(): jnp.zeros((channels, tile_rows * tile_cols), jnp.float32).at[:, cell_ids]]
    gather x4 -> x0, local copies, waits for them, and re-layouts: 80.1 us -> none  [the longest x1 57.6 us: per_device(): local_fit = diffused.reshape(channels, -1)[:, cell_ids]]
    ppermute x14 -> x0, waiting for transfers between devices: 39.6 us -> none  [the longest x7 25.6 us: with_halo(): lax.ppermute(lax.slice_in_dim(block, 0, width, axis=dim), axis, backward)]
    all_to_all x1 -> x0, blocking collectives: 32.2 us -> none  [per_device(): lax.all_to_all(local_fit.reshape(1, channels, devices, slots), ('lat', 'l...]
    all_to_all x2 -> x0, waiting for transfers between devices: 31.2 us -> none  [the longest x1 24.4 us: per_device(): lax.all_to_all(outgoing, ('lat', 'lon'), split_axis=2, concat_axis=2, til...]
    all_gather x3 -> x0, local copies, waits for them, and re-layouts: 29.2 us -> none  [extend_deep(): lax.all_gather(block[:, tile_rows - depth:, :], 'lon', axis=2, tiled=True)]
  transfers between devices with their start and end apart: 19 -> 0, of which waited for: 9 -> 0; matrix products, arithmetic and copies ran while one was open for 29% -> 0% of each run, Pallas kernels for 0% -> 0%
where the time goes in v1:
time: 227 us
  Pallas kernels  214 us (94%)
  local copies, waits for them, and re-layouts  9.25 us (4%)
  other arithmetic  3.03 us (1%)
    pallas_call x1, Pallas kernels, gather(): pl.pallas_call(functools.partial(gather_kernel, n, n_lon, size), out_shap...  90.3 us
    pallas_call x1, Pallas kernels, diffuse(): pl.pallas_call(functools.partial(diffuse_kernel, n_lat, n_lon), out_shape...  68.7 us
    pallas_call x1, Pallas kernels, scatter(): pl.pallas_call(functools.partial(scatter_kernel, n, n_lon, size), out_sha...  55 us

profile of v1, /device:TPU:0, one launch (start us, length us, event | category | flops | bytes accessed | tf_op | source)
XLA Modules:
  0.0 226.9 jit_solution(12688042404196584617)
XLA Ops:
  0.6 0.0 copy-start
  0.6 0.7 pad_bitcast_fusion.1
  1.3 0.7 pad_bitcast_fusion
  2.0 0.7 copy.15.sigma_ref
  2.7 0.7 copy.14.scale_ref
  3.4 0.8 convert_element_type.10
  4.2 1.6 fusion.cell_ref
  5.8 0.0 copy-done
  5.8 0.7 maximum_bitcast_fusion.coef_ref
  6.5 55.0 %scatter.1 = (f32[2,48,24,128]{3,2,1,0:T(8,128)}, f32[128,128]{1,0:T(8,128)}) custom-call(f32[21,128,128]{2,1,0:T(8,128)} %bitcast.21, f32[128,128]{1,0:T(8,128)} %fusion.cell_ref), custom_call_target="tpu_custom_call" | custom-call | tf_op jit(solution)/shard_map/scatter/pallas_call | solution.py:142
  61.4 68.7 %diffuse.1.state_ref = f32[2,48,24,128]{3,2,1,0:T(8,128)} custom-call(s32[256]{0:T(256)} %partner_ref.1, f32[2,48,24,128]{3,2,1,0:T(8,128)} %get-tuple-element.5.field_ref, f32[2,3,48,128]{3,2,1,0:T(8,128)} %maximum_bitcast_fusion.coef_ref, f32[24,1]{1,0:T(8,128)} %copy.14.scale_ref, f32[24,1]{1,0:T(8,128)} %copy.15.sigma_ref), custom_call_target="tpu_custom_call" | custom-call | tf_op jit(solution)/shard_map/diffuse/pallas_call | solution.py:477
  130.1 1.3 slice_bitcast_fusion
  131.5 0.8 copy.16
  132.3 1.8 reshape.12
  134.0 90.3 %gather.1 = f32[21,128,128]{2,1,0:T(8,128)} custom-call(f32[128,128]{1,0:T(8,128)} %get-tuple-element.4.slot_ref, f32[2,48,24,128]{3,2,1,0:T(8,128)} %diffuse.1.state_ref), custom_call_target="tpu_custom_call" | custom-call | tf_op jit(solution)/shard_map/gather/pallas_call | solution.py:580
  224.4 2.6 %copy.20 = f32[1,21,128,128]{3,2,1,0:T(8,128)} copy(f32[1,21,128,128]{3,2,1,0:T(8,128)} %bitcast.20) | data formatting | bytes 2752512
  (3 shorter events, 0.0 us)
Async XLA Ops:
  0.6 5.1 %copy-start = (f32[2,48,256]{2,1,0:T(8,128)S(1)}, f32[2,48,256]{2,1,0:T(8,128)}, u32[]{:S(2)}) copy-start(f32[2,48,256]{2,1,0:T(8,128)} %param.12) | copy-start | bytes 294916

commit v2 on v0

v2 whole, which is shorter than its diff:
```python
import functools

import jax
import jax.numpy as jnp
from jax import lax
from jax.experimental import pallas as pl
from jax.experimental.pallas import tpu as pltpu
from jax.sharding import PartitionSpec as P

LEV = 10
C = 21
CP = 24
ROWS = 48
COLS = 256
BAND = ROWS // 2
PLACES = 2 * COLS
DEEP = 12
EXT = ROWS + 2 * DEEP
GRP = 16
CEXT = ROWS + 2 * GRP
F32 = jnp.float32
BF16 = jnp.bfloat16
MESH = pl.DeviceIdType.MESH
VMEM_LIMIT = 60 * 2**20


def place_of(linear, n_lon):
    return (linear // n_lon, lax.rem(linear, n_lon))


def split(cell):
    cell = cell.astype(jnp.int32)
    place = cell & (PLACES - 1)
    low = place & 255
    half = place >> 8
    return cell >> 9, [jnp.where(half == h, low, 512).astype(F32) for h in range(2)]


def store_onehot(onehot, halves, lanes):
    one = jnp.ones((16, 128), BF16)
    zero = jnp.zeros((16, 128), BF16)
    steps = lax.broadcasted_iota(jnp.int32, (16, 128), 0).astype(F32).astype(BF16)
    for h in range(2):
        row = jnp.broadcast_to(halves[h], (16, 128)).astype(BF16)
        for t in range(16):
            first = h * 256 + t * 16
            onehot[first : first + 16, lanes] = jnp.where(row == steps + BF16(16 * t), one, zero)


def build_chunk(arrived, chunk, size, lhs, onehot):
    for j in range(size):
        value = arrived[chunk * size + j]
        band, halves = split(value[C : C + 1, :])
        lanes = slice(j * 128, (j + 1) * 128)
        high = value.astype(BF16)
        pieces = jnp.concatenate([value, value - high.astype(F32)], axis=0).astype(BF16)
        band = jnp.broadcast_to(band.astype(F32), (16, 128)).astype(BF16)
        zero = jnp.zeros((2 * CP, 128), BF16)
        for b in range(BAND):
            mask = jnp.concatenate([band == BF16(b)] * 3, axis=0)
            lhs[b * 2 * CP : (b + 1) * 2 * CP, lanes] = jnp.where(mask, pieces, zero)
        store_onehot(onehot, halves, lanes)


def lanes_of(shape):
    return lax.broadcasted_iota(jnp.int32, shape, len(shape) - 1)


def east_of(tiles):
    turned = [pltpu.roll(x, 127, x.ndim - 1) for x in tiles]
    last = lanes_of(tiles[0].shape) == 127
    return [jnp.where(last, turned[(t + 1) % 3], turned[t]) for t in range(3)]


def west_of(tiles):
    turned = [pltpu.roll(x, 1, x.ndim - 1) for x in tiles]
    first = lanes_of(tiles[0].shape) == 0
    return [jnp.where(first, turned[(t + 2) % 3], turned[t]) for t in range(3)]


def sweep(source, target, rhs, weights, first, stop, unroll):
    w_e, w_w, w_n, w_s = weights
    unroll = min(unroll, stop - first)

    def block(i, carry):
        start = jnp.minimum(first + i * unroll, stop - unroll)
        for c in range(0, CP, 8):
            part = pl.ds(c, 8)
            below = [source[t, start - 1, part] for t in range(3)]
            here = [source[t, start, part] for t in range(3)]
            for k in range(unroll):
                r = start + k
                above = [source[t, r + 1, part] for t in range(3)]
                to_east, to_west = east_of(here), west_of(here)
                for t in range(3):
                    target[t, r, part] = (
                        (rhs[t, r, part] + w_n[t, r, part] * above[t])
                        + (w_s[t, r, part] * below[t] + w_e[t, r, part] * to_east[t])
                        + w_w[t, r, part] * to_west[t]
                    )
                below, here = here, above
        return carry

    lax.fori_loop(0, -(-(stop - first) // unroll), block, 0)


def kernel(
    n_lat, n_lon, size, back, partner_ref, value_ref, cell_ref, coef_ref, scale_ref, sigma_ref, out_ref, state_ref,
    outgoing, arrived, lhs0, onehot0, lhs1, onehot1, total, field, fits, pieces,
    cur, nxt, rhs, inv, w_e, w_w, w_n, w_s, pack_e, pack_w, edge_e, edge_w,
    coef, coef_e, coef_w, fold, coef_fold,
    local_sem, obs_send, obs_recv, way_send, way_recv, fold_send, fold_recv, back_send, back_recv,
):
    n = n_lat * n_lon
    lat = lax.axis_index("lat")
    lon = lax.axis_index("lon")
    me = lat * n_lon + lon
    top = lat == n_lat - 1
    load = pltpu.make_async_copy(value_ref, outgoing.at[0:C], local_sem.at[0])
    load.start()
    barrier = pltpu.get_barrier_semaphore()

    def greet(i, carry):
        pl.semaphore_signal(barrier, inc=1, device_id=place_of(lax.rem(me + i, n), n_lon), device_id_type=MESH)
        return carry

    @pl.when(lat == 0)
    def _():
        cur[0:2, 0:DEEP] = jnp.zeros((2, DEEP, CP, 128), F32)
        edge_e[0:2] = jnp.zeros((2, CP, 128), F32)
        edge_w[0:2] = jnp.zeros((2, CP, 128), F32)
        coef[:, :, 0:GRP, :] = jnp.zeros((2, 3, GRP, 128), F32)
        coef_e[:, 0:GRP, :] = jnp.zeros((3, GRP, 128), F32)
        coef_w[:, 0:GRP, :] = jnp.zeros((3, GRP, 128), F32)

    @pl.when(top)
    def _():
        edge_e[8:10] = jnp.zeros((2, CP, 128), F32)
        edge_w[8:10] = jnp.zeros((2, CP, 128), F32)
        coef_e[:, GRP + ROWS : CEXT, :] = jnp.zeros((3, GRP, 128), F32)
        coef_w[:, GRP + ROWS : CEXT, :] = jnp.zeros((3, GRP, 128), F32)

    lax.fori_loop(1, n, greet, 0)
    outgoing[C] = cell_ref[...]
    total[...] = jnp.zeros_like(total)
    for t in range(2):
        coef[t, :, GRP : GRP + ROWS, :] = coef_ref[t]
    load.wait()
    pl.semaphore_wait(barrier, n - 1)

    east = lax.rem(lon + 1, n_lon)
    west = lax.rem(lon + n_lon - 1, n_lon)
    has_n = lat < n_lat - 1
    has_s = lat > 0
    everywhere = lat >= 0
    north = jnp.minimum(lat + 1, n_lat - 1)
    south = jnp.maximum(lat - 1, 0)
    ways = [
        (everywhere, lat, east, everywhere),
        (everywhere, lat, west, everywhere),
        (has_n, north, lon, has_s),
        (has_n, north, east, has_s),
        (has_n, north, west, has_s),
        (has_s, south, lon, has_n),
        (has_s, south, east, has_n),
        (has_s, south, west, has_n),
    ]
    mid_g, low_g, high_g = pl.ds(GRP, ROWS), pl.ds(0, GRP), pl.ds(GRP + ROWS, GRP)
    head, tail = pl.ds(0, GRP), pl.ds(ROWS - GRP, GRP)
    copies = [
        ((pack_e, edge_w.at[pl.ds(2, 6)]), (coef_ref.at[1], coef_w.at[:, mid_g, :])),
        ((pack_w, edge_e.at[pl.ds(2, 6)]), (coef_ref.at[0], coef_e.at[:, mid_g, :])),
        (
            (field.at[:, pl.ds(ROWS - DEEP, DEEP)], cur.at[pl.ds(0, 2), pl.ds(0, DEEP)]),
            (coef_ref.at[:, :, tail, :], coef.at[:, :, low_g, :]),
        ),
        ((pack_e.at[pl.ds(4, 2)], edge_w.at[pl.ds(0, 2)]), (coef_ref.at[1, :, tail, :], coef_w.at[:, low_g, :])),
        ((pack_w.at[pl.ds(4, 2)], edge_e.at[pl.ds(0, 2)]), (coef_ref.at[0, :, tail, :], coef_e.at[:, low_g, :])),
        (
            (field.at[:, pl.ds(0, DEEP)], cur.at[pl.ds(0, 2), pl.ds(EXT - DEEP, DEEP)]),
            (coef_ref.at[:, :, head, :], coef.at[:, :, high_g, :]),
        ),
        ((pack_e.at[pl.ds(0, 2)], edge_w.at[pl.ds(8, 2)]), (coef_ref.at[1, :, head, :], coef_w.at[:, high_g, :])),
        ((pack_w.at[pl.ds(0, 2)], edge_e.at[pl.ds(8, 2)]), (coef_ref.at[0, :, head, :], coef_e.at[:, high_g, :])),
    ]

    def copy_of(w, k):
        source, target = copies[w][k]
        return pltpu.make_async_remote_copy(
            src_ref=source,
            dst_ref=target,
            send_sem=way_send.at[w, k],
            recv_sem=way_recv.at[w, k],
            device_id=(ways[w][1], ways[w][2]),
            device_id_type=MESH,
        )

    def start_ways(k):
        for w in range(8):
            @pl.when(ways[w][0])
            def _():
                copy_of(w, k).start()

    def wait_ways(k, which):
        for w in which:
            @pl.when(ways[w][3])
            def _():
                copy_of(w, k).wait_recv()

    def drain_ways(k):
        for w in range(8):
            @pl.when(ways[w][0])
            def _():
                copy_of(w, k).wait_send()

    mine = pl.ds(2 * lon, 2)
    folds = [
        (field.at[:, pl.ds(ROWS - DEEP, DEEP)], fold),
        (coef_ref.at[:, :, tail, :], coef_fold),
    ]

    def fold_copy(k, i):
        source, target = folds[k]
        return pltpu.make_async_remote_copy(
            src_ref=source,
            dst_ref=target.at[mine],
            send_sem=fold_send.at[k, i],
            recv_sem=fold_recv.at[k, i],
            device_id=(lat, lax.rem(lon + i, n_lon)),
            device_id_type=MESH,
        )

    def start_fold(k):
        def one(i, carry):
            fold_copy(k, i).start()
            return carry

        lax.fori_loop(1, n_lon, one, 0)
        own = pltpu.make_async_copy(folds[k][0], folds[k][1].at[mine], local_sem.at[1])
        own.start()
        own.wait()

    def wait_fold(k):
        def one(i, carry):
            fold_copy(k, i).wait()
            return carry

        lax.fori_loop(1, n_lon, one, 0)

    corner = partner_ref[0]
    tile0 = corner // 128
    shift = lax.rem(corner, 128)
    places = [lax.rem(tile0 + x - 4 + 2 * n_lon, 2 * n_lon) for x in range(1, 6)]

    def mirrored(load, rows):
        lane = lanes_of((rows, 128))
        index = (shift - lane) & 127
        near = lane <= shift
        tiles = [jnp.take_along_axis(load(p), index, axis=1) for p in places]
        merged = [jnp.where(near, tiles[x], tiles[x - 1]) for x in range(1, 5)]
        return merged[2], merged[1], jnp.where(lane < 64, merged[0], merged[3])

    start_ways(1)

    @pl.when(top)
    def _():
        start_fold(1)

    def send(i, carry):
        owner = lax.rem(me + i, n)
        pltpu.make_async_remote_copy(
            src_ref=outgoing.at[:, owner, :],
            dst_ref=arrived.at[i, 0 : C + 1, :],
            send_sem=obs_send,
            recv_sem=obs_recv.at[i // size],
            device_id=place_of(owner, n_lon),
            device_id_type=MESH,
        ).start()
        return carry

    own_obs = pltpu.make_async_copy(outgoing.at[:, me, :], arrived.at[0, 0 : C + 1, :], local_sem.at[0])
    own_obs.start()
    lax.fori_loop(1, n, send, 0)

    wait_ways(1, range(8))
    side_c = lanes_of((3, CEXT, 128)) < 64
    coef_e[...] = jnp.where(side_c, coef_e[...], coef_w[...])

    @pl.when(top)
    def _():
        wait_fold(1)
        for k in range(3):
            tiles = mirrored(lambda p: coef_fold[p, k], GRP)
            for d in range(GRP):
                row = GRP + ROWS + d
                for t in range(2):
                    coef[t, k, row : row + 1, :] = tiles[t][GRP - 1 - d : GRP - d]
                coef_e[k, row : row + 1, :] = tiles[2][GRP - 1 - d : GRP - d]

    channel = lax.broadcasted_iota(jnp.int32, (CP, 128), 0)
    level = jnp.where(channel < LEV, channel, jnp.where(channel < 2 * LEV, channel - LEV, 0))
    level = jnp.where(channel < C, level, 2 * LEV).astype(F32)
    scale = jnp.broadcast_to(scale_ref[...], (CP, 128))
    sigma = jnp.broadcast_to(sigma_ref[...], (CP, 128))

    def coef_row(k, row):
        return [
            jnp.broadcast_to(ref[k, pl.ds(row, 1), :], (CP, 128))
            for ref in (coef.at[0], coef.at[1], coef_e)
        ]

    def weigh(r, carry):
        g = r + (GRP - DEEP)
        deep, deep_n, deep_s = coef_row(0, g), coef_row(0, g + 1), coef_row(0, g - 1)
        k0 = coef_row(1, g)
        k1, k1_n, k1_s = coef_row(2, g), coef_row(2, g + 1), coef_row(2, g - 1)
        k0_east, k0_west = east_of(k0), west_of(k0)
        deep_east, deep_west = east_of(deep), west_of(deep)
        for t in range(3):
            def face(k, deep_there):
                both = level < jnp.minimum(deep[t], deep_there)
                return jnp.where(both, scale * (0.5 * k), 0.0)

            e = face(k0[t] + k0_east[t], deep_east[t])
            w = face(k0[t] + k0_west[t], deep_west[t])
            m = face(k1[t] + k1_n[t], deep_n[t])
            s = face(k1[t] + k1_s[t], deep_s[t])
            over = 1.0 / (1.0 + e + w + m + s)
            inv[t, r] = over
            w_e[t, r] = e * over
            w_w[t, r] = w * over
            w_n[t, r] = m * over
            w_s[t, r] = s * over
        return carry

    lax.fori_loop(0, EXT, weigh, 0)
    drain_ways(1)

    def arrive(chunk, first):
        window = arrived.at[pl.ds(chunk * size + first, size - first), 0 : C + 1, :]
        pltpu.make_async_copy(window, window, obs_recv.at[chunk]).wait()

    chunks = n // size
    dims = (((1,), (1,)), ((), ()))
    own_obs.wait()
    arrive(0, 1)
    build_chunk(arrived, 0, size, lhs0, onehot0)

    def pair(i, carry):
        arrive(2 * i + 1, 0)
        build_chunk(arrived, 2 * i + 1, size, lhs1, onehot1)
        total[...] += lax.dot_general(lhs0[...], onehot0[...], dims, preferred_element_type=F32)
        more = 2 * i + 2

        @pl.when(more < chunks)
        def _():
            arrive(more, 0)

        build_chunk(arrived, jnp.minimum(more, chunks - 1), size, lhs0, onehot0)
        total[...] += lax.dot_general(lhs1[...], onehot1[...], dims, preferred_element_type=F32)
        return carry

    lax.fori_loop(0, chunks // 2, pair, 0)
    for b in range(BAND):
        first = b * 2 * CP
        band = total[first : first + CP, :] + total[first + CP : first + 2 * CP, :]
        for t in range(4):
            field[t % 2, 2 * b + t // 2] = band[:, t * 128 : (t + 1) * 128]

    lane16 = lanes_of((CP, 128)) >> 4
    for i in range(ROWS // 8):
        first = jnp.zeros((CP, 128), F32)
        last = jnp.zeros((CP, 128), F32)
        for j in range(8):
            x = field[0, 8 * i + j]
            y = field[1, 8 * i + j]
            first = jnp.where(lane16 == j, pltpu.roll(x, 16 * j, 1) if j else x, first)
            last = jnp.where(lane16 == j, pltpu.roll(y, 16 * j + 16, 1) if j < 7 else y, last)
        pack_w[i] = first
        pack_e[i] = last

    start_ways(0)

    @pl.when(top)
    def _():
        start_fold(0)

    def begin(r, tiles):
        deep = coef_row(0, r + (GRP - DEEP))
        for t in range(3):
            start = jnp.where(level < deep[t], tiles[t] * sigma, 0.0)
            cur[t, r] = start
            rhs[t, r] = start * inv[t, r]

    side = lanes_of((CP, 128)) < 64

    def unpack(i):
        from_e = edge_e[i]
        from_w = edge_w[i]
        for j in range(8):
            x = pltpu.roll(from_e, 128 - 16 * j, 1) if j else from_e
            y = pltpu.roll(from_w, 112 - 16 * j, 1) if j < 7 else from_w
            row = 8 * i + j - (GRP - DEEP)
            if 0 <= row < EXT:
                cur[2, row] = jnp.where(side, x, y)

    def begin_own(r, carry):
        begin(r, [field[0, r - DEEP], field[1, r - DEEP], cur[2, r]])
        return carry

    def begin_ghost(r, carry):
        begin(r, [cur[t, r] for t in range(3)])
        return carry

    wait_ways(0, range(0, 5))
    for i in range(0, 8):
        unpack(i)
    lax.fori_loop(0, DEEP, begin_ghost, 0)
    lax.fori_loop(DEEP, DEEP + ROWS, begin_own, 0, unroll=2)

    weights = (w_e, w_w, w_n, w_s)
    buffers = [cur, nxt]

    def renew(first, stop):
        def one(r, carry):
            for t in range(3):
                rhs[t, r] = cur[t, r] * inv[t, r]
            return carry

        lax.fori_loop(first, stop, one, 0, unroll=2)

    limit = DEEP + ROWS
    for s in range(1, DEEP + 1):
        if s == DEEP // 2 + 1:
            renew(s, limit - s)
        sweep(buffers[(s - 1) % 2], buffers[s % 2], rhs, weights, s, limit - s, 12)

    wait_ways(0, range(5, 8))
    for i in range(8, 10):
        unpack(i)

    @pl.when(top)
    def _():
        wait_fold(0)

        def ghost(d, carry):
            tiles = mirrored(lambda p: fold[p, DEEP - 1 - d], CP)
            for t in range(3):
                cur[t, limit + d] = tiles[t]
            return carry

        lax.fori_loop(0, DEEP, ghost, 0)

    lax.fori_loop(limit, EXT, begin_ghost, 0)
    for s in range(1, DEEP + 1):
        if s == DEEP // 2 + 1:
            renew(limit - s, EXT - s)
        sweep(buffers[(s - 1) % 2], buffers[s % 2], rhs, weights, limit - s, EXT - s, 12)

    for b in range(0, BAND, 2):
        for half in range(2):
            for t in range(2):
                rows = []
                for row in (2 * b + half, 2 * b + 2 + half):
                    value = cur[t, row + DEEP] * sigma
                    state_ref[t, row] = value
                    rows.append(value)
                rows = jnp.concatenate(rows, axis=0)
                high = rows.astype(BF16)
                low = (rows - high.astype(F32)).astype(BF16)
                first = half * COLS + t * 128
                pieces[b * CP : (b + 2) * CP, first : first + 128] = high
                pieces[b * CP : (b + 2) * CP, PLACES + first : PLACES + first + 128] = low

    def chunk(g, carry):
        bands = []
        for j in range(back):
            band, halves = split(arrived[g * back + j, C : C + 1, :])
            bands.append(band)
            store_onehot(onehot0, halves, slice(j * 128, (j + 1) * 128))
        hot = onehot0[:, : back * 128]
        picked = jnp.dot(pieces[:, :PLACES], hot, preferred_element_type=F32) + jnp.dot(
            pieces[:, PLACES:], hot, preferred_element_type=F32
        )
        for j in range(back):
            band = jnp.broadcast_to(bands[j], (CP, 128))
            fit = jnp.zeros((CP, 128), F32)
            for b in range(BAND):
                fit += jnp.where(band == b, picked[b * CP : (b + 1) * CP, j * 128 : (j + 1) * 128], 0.0)
            fits[g * back + j] = fit
        for j in range(back):
            i = g * back + j
            to = lax.rem(me - i + n, n)

            @pl.when(i > 0)
            def _():
                pltpu.make_async_remote_copy(
                    src_ref=fits.at[i, 0:C, :],
                    dst_ref=out_ref.at[:, me, :],
                    send_sem=back_send,
                    recv_sem=back_recv,
                    device_id=place_of(to, n_lon),
                    device_id_type=MESH,
                ).start()

        return carry

    lax.fori_loop(0, n // back, chunk, 0)
    own_fit = pltpu.make_async_copy(fits.at[0, 0:C, :], out_ref.at[:, me, :], local_sem.at[0])
    own_fit.start()
    own_fit.wait()
    drain_ways(0)
    sent = arrived.at[1:n, 0 : C + 1, :]
    pltpu.make_async_copy(sent, sent, obs_send).wait()
    sent = fits.at[1:n, 0:C, :]
    pltpu.make_async_copy(sent, sent, back_send).wait()
    pltpu.make_async_copy(sent, sent, back_recv).wait()


def run(n_lat, n_lon, partner, value, cell, coef, scale, sigma):
    n = n_lat * n_lon
    size = min(8, n // 4)
    back = min(4, n // 4)
    vmem = pl.BlockSpec(memory_space=pltpu.VMEM)
    buffers = [
        pltpu.VMEM((BAND * 2 * CP, size * 128), BF16),
        pltpu.VMEM((PLACES, size * 128), BF16),
    ]
    state = pltpu.VMEM((3, EXT, CP, 128), F32)
    return pl.pallas_call(
        functools.partial(kernel, n_lat, n_lon, size, back),
        out_shape=(
            jax.ShapeDtypeStruct((C, n, 128), F32),
            jax.ShapeDtypeStruct((2, ROWS, CP, 128), F32),
        ),
        in_specs=[
            pl.BlockSpec(memory_space=pltpu.SMEM),
            pl.BlockSpec(memory_space=pl.ANY),
            vmem,
            vmem,
            vmem,
            vmem,
        ],
        out_specs=(vmem, vmem),
        scratch_shapes=[
            pltpu.VMEM((C + 1, n, 128), F32),
            pltpu.VMEM((n, CP, 128), F32),
            *buffers,
            *buffers,
            pltpu.VMEM((BAND * 2 * CP, PLACES), F32),
            pltpu.VMEM((2, ROWS, CP, 128), F32),
            pltpu.VMEM((n, CP, 128), F32),
            pltpu.VMEM((BAND * CP, 2 * PLACES), BF16),
            *[state] * 8,
            pltpu.VMEM((ROWS // 8, CP, 128), F32),
            pltpu.VMEM((ROWS // 8, CP, 128), F32),
            pltpu.VMEM((CEXT // 8, CP, 128), F32),
            pltpu.VMEM((CEXT // 8, CP, 128), F32),
            pltpu.VMEM((2, 3, CEXT, 128), F32),
            pltpu.VMEM((3, CEXT, 128), F32),
            pltpu.VMEM((3, CEXT, 128), F32),
            pltpu.VMEM((2 * n_lon, DEEP, CP, 128), F32),
            pltpu.VMEM((2 * n_lon, 3, GRP, 128), F32),
            pltpu.SemaphoreType.DMA((2,)),
            pltpu.SemaphoreType.DMA,
            pltpu.SemaphoreType.DMA((n // size,)),
            pltpu.SemaphoreType.DMA((8, 2)),
            pltpu.SemaphoreType.DMA((8, 2)),
            pltpu.SemaphoreType.DMA((2, n_lon)),
            pltpu.SemaphoreType.DMA((2, n_lon)),
            pltpu.SemaphoreType.DMA,
            pltpu.SemaphoreType.DMA,
        ],
        compiler_params=pltpu.CompilerParams(
            collective_id=0, has_side_effects=True, vmem_limit_bytes=VMEM_LIMIT
        ),
        name="covariance",
    )(partner, value, cell, coef, scale, sigma)


def per_device(
    n_lat, n_lon, obs_value, obs_cell, obs_count, bottom_level, diffusivity, partner, length_scale, sigma
):
    n = n_lat * n_lon
    slots = lax.broadcasted_iota(jnp.int32, (n, 128), 1)
    cell = jnp.where(slots < obs_count[0][:, None], obs_cell[0], -1).astype(F32)
    coef = jnp.concatenate([bottom_level.astype(F32)[None], diffusivity], axis=0)
    coef = coef.reshape(3, ROWS, 2, 128).transpose(2, 0, 1, 3)
    column = lambda x: jnp.pad(x, (0, CP - C))[:, None]
    fit, state = run(
        n_lat, n_lon, partner, obs_value[0], cell, coef, column(length_scale), column(sigma)
    )
    diffused = state[:, :, :C, :].transpose(2, 1, 0, 3).reshape(C, ROWS, COLS)
    return fit[None], diffused


def solution(mesh):
    n_lat, n_lon = mesh.shape["lat"], mesh.shape["lon"]
    return jax.shard_map(
        functools.partial(per_device, n_lat, n_lon),
        mesh=mesh,
        in_specs=(
            P(("lat", "lon"), None, None, None),
            P(("lat", "lon"), None, None),
            P(("lat", "lon"), None),
            P("lat", "lon"),
            P(None, "lat", "lon"),
            P("lon"),
            P(),
            P(),
        ),
        out_specs=(P(("lat", "lon"), None, None, None), P(None, "lat", "lon")),
        check_vma=False,
    )
```

time: 606 us -> 185 us (0.31); the launches traced: 597 us -> 185 us
  other arithmetic: 253 us -> 3.06 us
  Pallas kernels: 0 us -> 173 us
  local copies, waits for them, and re-layouts: 169 us -> 7.77 us
  waiting for transfers between devices: 85.9 us -> 0 us
  starting transfers between devices: 41.7 us -> 0 us
  blocking collectives: 32.2 us -> 0 us
  between operations: 14.8 us -> 0.68 us
    pallas_call x0 -> x1, Pallas kernels: none -> 173 us  [run(): pl.pallas_call(functools.partial(kernel, n_lat, n_lon, size, back), out_s...]
    div x11 -> x0, other arithmetic: 120 us -> none  [per_device(): (trim_margin(source_wide, depth, inner) + trim_margin(w_east, depth, inne...]
    scatter-add x1 -> x0, other arithmetic: 90.6 us -> none  [per_device(): jnp.zeros((channels, tile_rows * tile_cols), jnp.float32).at[:, cell_ids]]
    gather x4 -> x0, local copies, waits for them, and re-layouts: 80.1 us -> none  [the longest x1 57.6 us: per_device(): local_fit = diffused.reshape(channels, -1)[:, cell_ids]]
    ppermute x14 -> x0, waiting for transfers between devices: 39.6 us -> none  [the longest x7 25.6 us: with_halo(): lax.ppermute(lax.slice_in_dim(block, 0, width, axis=dim), axis, backward)]
    all_to_all x1 -> x0, blocking collectives: 32.2 us -> none  [per_device(): lax.all_to_all(local_fit.reshape(1, channels, devices, slots), ('lat', 'l...]
    all_to_all x2 -> x0, waiting for transfers between devices: 31.2 us -> none  [the longest x1 24.4 us: per_device(): lax.all_to_all(outgoing, ('lat', 'lon'), split_axis=2, concat_axis=2, til...]
    all_gather x3 -> x0, local copies, waits for them, and re-layouts: 29.2 us -> none  [extend_deep(): lax.all_gather(block[:, tile_rows - depth:, :], 'lon', axis=2, tiled=True)]
  transfers between devices with their start and end apart: 19 -> 0, of which waited for: 9 -> 0; matrix products, arithmetic and copies ran while one was open for 29% -> 0% of each run, Pallas kernels for 0% -> 0%
where the time goes in v2:
time: 185 us
  Pallas kernels  173 us (94%)
  local copies, waits for them, and re-layouts  7.77 us (4%)
  other arithmetic  3.06 us (2%)
    pallas_call x1, Pallas kernels, run(): pl.pallas_call(functools.partial(kernel, n_lat, n_lon, size, back), out_s...  173 us

profile of v2, /device:TPU:0, one launch (start us, length us, event | category | flops | bytes accessed | tf_op | source)
XLA Modules:
  0.0 184.8 jit_solution(9664417339935179447)
XLA Ops:
  0.6 0.0 copy-start
  0.6 0.8 convert_element_type.10
  1.5 0.0 copy-done
  1.6 0.7 maximum_bitcast_fusion.coef_ref
  2.2 1.6 fusion.cell_ref
  3.8 0.7 pad_bitcast_fusion.1
  4.4 0.7 copy.14.scale_ref
  5.1 0.7 pad_bitcast_fusion
  5.8 0.7 copy.15.sigma_ref
  6.5 173.3 %covariance.1 = (f32[21,128,128]{2,1,0:T(8,128)}, f32[2,48,24,128]{3,2,1,0:T(8,128)}) custom-call(s32[256]{0:T(256)} %partner_ref.1, f32[21,128,128]{2,1,0:T(8,128)} %bitcast.20, f32[128,128]{1,0:T(8,128)} %fusion.cell_ref, f32[2,3,48,128]{3,2,1,0:T(8,128)} %maximum_bitcast_fusion.coef_ref, f32[24,1]{1,0:T(8,128)} %copy.14.scale_ref, f32[24,1]{1,0:T(8,128)} %copy.15.sigma_ref), custom_call_target="tpu_custom_call" | custom-call | tf_op jit(solution)/shard_map/covariance/pallas_call | solution.py:530
  179.7 1.3 slice_bitcast_fusion
  181.1 0.8 copy.16
  181.9 0.0 copy-start.1
  181.9 1.8 reshape.12
  183.7 0.0 copy-done.1
  183.7 1.1 copy.20
  (3 shorter events, 0.0 us)
Async XLA Ops:
  0.6 0.9 copy-start
  181.9 1.8 copy-start.1

commit v3 on v2

--- a/solution.py
+++ b/solution.py
@@ -8,6 +8,7 @@
 from jax.sharding import PartitionSpec as P
 
 LEV = 10
+SWEEPS = 6
 C = 21
 CP = 24
 ROWS = 48
@@ -80,7 +81,6 @@
 
 def sweep(source, target, rhs, weights, first, stop, unroll):
     w_e, w_w, w_n, w_s = weights
-    unroll = min(unroll, stop - first)
 
     def block(i, carry):
         start = jnp.minimum(first + i * unroll, stop - unroll)
@@ -101,15 +101,17 @@
                 below, here = here, above
         return carry
 
-    lax.fori_loop(0, -(-(stop - first) // unroll), block, 0)
+    lax.fori_loop(0, (stop - first + unroll - 1) // unroll, block, 0)
 
 
 def kernel(
-    n_lat, n_lon, size, back, partner_ref, value_ref, cell_ref, coef_ref, scale_ref, sigma_ref, out_ref, state_ref,
-    outgoing, arrived, lhs0, onehot0, lhs1, onehot1, total, field, fits, pieces,
+    n_lat, n_lon, size, back,
+    partner_ref, count_ref, scale_ref, sigma_ref, value_ref, cell_ref, bottom_ref, diffusivity_ref, out_ref, state_ref,
+    outgoing, arrived, lhs0, onehot0, lhs1, onehot1, total, field, fits, pieces, picked0, picked1, coef_ref,
     cur, nxt, rhs, inv, w_e, w_w, w_n, w_s, pack_e, pack_w, edge_e, edge_w,
-    coef, coef_e, coef_w, fold, coef_fold,
-    local_sem, obs_send, obs_recv, way_send, way_recv, fold_send, fold_recv, back_send, back_recv,
+    coef, coef_e, coef_w, fold, coef_fold, mirror,
+    local_sem, obs_send, obs_recv, way_send, way_recv, fold_send, fold_recv, relay_send, relay_recv,
+    back_send, back_recv,
 ):
     n = n_lat * n_lon
     lat = lax.axis_index("lat")
@@ -141,10 +143,21 @@
         coef_w[:, GRP + ROWS : CEXT, :] = jnp.zeros((3, GRP, 128), F32)
 
     lax.fori_loop(1, n, greet, 0)
-    outgoing[C] = cell_ref[...]
+    lane_row = lanes_of((1, 128))
+
+    def mask_cells(o, carry):
+        row = cell_ref[pl.ds(o, 1), :]
+        outgoing[C, pl.ds(o, 1), :] = jnp.where(lane_row < count_ref[0, o], row, -1).astype(F32)
+        return carry
+
+    lax.fori_loop(0, n, mask_cells, 0, unroll=8)
+    for t in range(2):
+        lanes = slice(t * 128, (t + 1) * 128)
+        coef_ref[t, 0] = bottom_ref[:, lanes].astype(F32)
+        coef_ref[t, 1] = diffusivity_ref[0, :, lanes]
+        coef_ref[t, 2] = diffusivity_ref[1, :, lanes]
+        coef[t, :, GRP : GRP + ROWS, :] = coef_ref[t]
     total[...] = jnp.zeros_like(total)
-    for t in range(2):
-        coef[t, :, GRP : GRP + ROWS, :] = coef_ref[t]
     load.wait()
     pl.semaphore_wait(barrier, n - 1)
 
@@ -213,14 +226,14 @@
             def _():
                 copy_of(w, k).wait_send()
 
+    planes = n_lat // 2
+    share = DEEP // planes
+    plane = lat // 2
+    relays = lax.rem(lat, 2) == 1
     mine = pl.ds(2 * lon, 2)
-    folds = [
-        (field.at[:, pl.ds(ROWS - DEEP, DEEP)], fold),
-        (coef_ref.at[:, :, tail, :], coef_fold),
-    ]
-
-    def fold_copy(k, i):
-        source, target = folds[k]
+
+    def lon_copy(k, i):
+        source, target = ((fold.at[mine], fold), (coef_ref.at[:, :, tail, :], coef_fold))[k]
         return pltpu.make_async_remote_copy(
             src_ref=source,
             dst_ref=target.at[mine],
@@ -230,22 +243,94 @@
             device_id_type=MESH,
         )
 
-    def start_fold(k):
+    def start_lon(k):
         def one(i, carry):
-            fold_copy(k, i).start()
+            lon_copy(k, i).start()
             return carry
 
         lax.fori_loop(1, n_lon, one, 0)
-        own = pltpu.make_async_copy(folds[k][0], folds[k][1].at[mine], local_sem.at[1])
-        own.start()
-        own.wait()
-
-    def wait_fold(k):
+
+    def wait_lon(k):
         def one(i, carry):
-            fold_copy(k, i).wait()
+            lon_copy(k, i).wait()
             return carry
 
         lax.fori_loop(1, n_lon, one, 0)
+
+    def share_of(x):
+        return field.at[:, pl.ds(ROWS - DEEP + share * x, share)]
+
+    def to_relay(x):
+        return pltpu.make_async_remote_copy(
+            src_ref=share_of(x),
+            dst_ref=fold.at[mine],
+            send_sem=relay_send.at[0, x],
+            recv_sem=relay_recv.at[0, 0],
+            device_id=(2 * x + 1, lon),
+            device_id_type=MESH,
+        )
+
+    def from_relay(x):
+        return pltpu.make_async_remote_copy(
+            src_ref=mirror,
+            dst_ref=cur.at[:, pl.ds(EXT - share * (x + 1), share)],
+            send_sem=relay_send.at[1, 0],
+            recv_sem=relay_recv.at[1, x],
+            device_id=(n_lat - 1, lon),
+            device_id_type=MESH,
+        )
+
+    def own_share():
+        return pltpu.make_async_copy(share_of(planes - 1), fold.at[mine], local_sem.at[1])
+
+    def relay_out():
+        @pl.when(top)
+        def _():
+            for x in range(planes - 1):
+                to_relay(x).start()
+            own_share().start()
+            own_share().wait()
+
+        @pl.when(jnp.logical_and(relays, lat < n_lat - 1))
+        def _():
+            to_relay(0).wait_recv()
+
+        @pl.when(relays)
+        def _():
+            start_lon(0)
+
+    def relay_back():
+        @pl.when(relays)
+        def _():
+            wait_lon(0)
+            for d in range(share):
+                tiles = mirrored(lambda p: fold[p, share - 1 - d], CP)
+                for t in range(3):
+                    mirror[t, d] = tiles[t]
+
+        for x in range(planes - 1):
+            @pl.when(jnp.logical_and(relays, plane == x))
+            def _():
+                from_relay(x).start()
+
+        @pl.when(top)
+        def _():
+            own = pltpu.make_async_copy(mirror, cur.at[:, pl.ds(EXT - DEEP, share)], local_sem.at[1])
+            own.start()
+            own.wait()
+            for x in range(planes - 1):
+                to_relay(x).wait_send()
+
+    def relay_end():
+        @pl.when(top)
+        def _():
+            for x in range(planes - 1):
+                from_relay(x).wait_recv()
+
+        for x in range(planes - 1):
+            @pl.when(jnp.logical_and(relays, plane == x))
+            def _():
+                from_relay(x).wait_send()
 
     corner = partner_ref[0]
     tile0 = corner // 128
@@ -264,7 +349,10 @@
 
     @pl.when(top)
     def _():
-        start_fold(1)
+        start_lon(1)
+        own = pltpu.make_async_copy(coef_ref.at[:, :, tail, :], coef_fold.at[mine], local_sem.at[1])
+        own.start()
+        own.wait()
 
     def send(i, carry):
         owner = lax.rem(me + i, n)
@@ -272,15 +360,19 @@
             src_ref=outgoing.at[:, owner, :],
             dst_ref=arrived.at[i, 0 : C + 1, :],
             send_sem=obs_send,
-            recv_sem=obs_recv.at[i // size],
+            recv_sem=obs_recv.at[i // (2 * size)],
             device_id=place_of(owner, n_lon),
             device_id_type=MESH,
         ).start()
         return carry
 
+    early = n // 4
+    beside = n // 2
+    rest = n - early - beside
+
     own_obs = pltpu.make_async_copy(outgoing.at[:, me, :], arrived.at[0, 0 : C + 1, :], local_sem.at[0])
     own_obs.start()
-    lax.fori_loop(1, n, send, 0)
+    lax.fori_loop(1, early, send, 0)
 
     wait_ways(1, range(8))
     side_c = lanes_of((3, CEXT, 128)) < 64
@@ -288,7 +380,7 @@
 
     @pl.when(top)
     def _():
-        wait_fold(1)
+        wait_lon(1)
         for k in range(3):
             tiles = mirrored(lambda p: coef_fold[p, k], GRP)
             for d in range(GRP):
@@ -300,8 +392,11 @@
     channel = lax.broadcasted_iota(jnp.int32, (CP, 128), 0)
     level = jnp.where(channel < LEV, channel, jnp.where(channel < 2 * LEV, channel - LEV, 0))
     level = jnp.where(channel < C, level, 2 * LEV).astype(F32)
-    scale = jnp.broadcast_to(scale_ref[...], (CP, 128))
-    sigma = jnp.broadcast_to(sigma_ref[...], (CP, 128))
+    scale = jnp.zeros((CP, 128), F32)
+    sigma = jnp.zeros((CP, 128), F32)
+    for c in range(C):
+        scale = jnp.where(channel == c, scale_ref[c], scale)
+        sigma = jnp.where(channel == c, sigma_ref[c], sigma)
 
     def coef_row(k, row):
         return [
@@ -333,34 +428,43 @@
             w_s[t, r] = s * over
         return carry
 
-    lax.fori_loop(0, EXT, weigh, 0)
+    def weigh_and_send(r, carry):
+        send(early + r, carry)
+        return weigh(r, carry)
+
+    lax.fori_loop(0, beside, weigh_and_send, 0)
+    lax.fori_loop(beside, EXT, weigh, 0)
     drain_ways(1)
 
-    def arrive(chunk, first):
-        window = arrived.at[pl.ds(chunk * size + first, size - first), 0 : C + 1, :]
-        pltpu.make_async_copy(window, window, obs_recv.at[chunk]).wait()
-
-    chunks = n // size
+    def arrive(group, first):
+        window = arrived.at[pl.ds(group * 2 * size + first, 2 * size - first), 0 : C + 1, :]
+        pltpu.make_async_copy(window, window, obs_recv.at[group]).wait()
+
+    pairs = n // size // 2
     dims = (((1,), (1,)), ((), ()))
+    batch = -(-rest // (pairs - 1))
+
+    def accumulate(lhs, onehot):
+        total[...] += lax.dot_general(lhs[...], onehot[...], dims, preferred_element_type=F32)
+
     own_obs.wait()
     arrive(0, 1)
     build_chunk(arrived, 0, size, lhs0, onehot0)
 
     def pair(i, carry):
-        arrive(2 * i + 1, 0)
+        first = early + beside + i * batch
+        lax.fori_loop(first, jnp.minimum(first + batch, n), send, 0)
+        arrive(i + 1, 0)
         build_chunk(arrived, 2 * i + 1, size, lhs1, onehot1)
-        total[...] += lax.dot_general(lhs0[...], onehot0[...], dims, preferred_element_type=F32)
-        more = 2 * i + 2
-
-        @pl.when(more < chunks)
-        def _():
-            arrive(more, 0)
-
-        build_chunk(arrived, jnp.minimum(more, chunks - 1), size, lhs0, onehot0)
-        total[...] += lax.dot_general(lhs1[...], onehot1[...], dims, preferred_element_type=F32)
-        return carry
-
-    lax.fori_loop(0, chunks // 2, pair, 0)
+        accumulate(lhs0, onehot0)
+        build_chunk(arrived, 2 * i + 2, size, lhs0, onehot0)
+        accumulate(lhs1, onehot1)
+        return carry
+
+    lax.fori_loop(0, pairs - 1, pair, 0)
+    build_chunk(arrived, 2 * pairs - 1, size, lhs1, onehot1)
+    accumulate(lhs0, onehot0)
+    accumulate(lhs1, onehot1)
     for b in range(BAND):
         first = b * 2 * CP
         band = total[first : first + CP, :] + total[first + CP : first + 2 * CP, :]
@@ -381,9 +485,7 @@
 
     start_ways(0)
 
-    @pl.when(top)
-    def _():
-        start_fold(0)
+    relay_out()
 
     def begin(r, tiles):
         deep = coef_row(0, r + (GRP - DEEP))
@@ -419,8 +521,6 @@
     lax.fori_loop(DEEP, DEEP + ROWS, begin_own, 0, unroll=2)
 
     weights = (w_e, w_w, w_n, w_s)
-    buffers = [cur, nxt]
-
     def renew(first, stop):
         def one(r, carry):
             for t in range(3):
@@ -429,83 +529,104 @@
 
         lax.fori_loop(first, stop, one, 0, unroll=2)
 
+    def sweeps(step, low, high):
+        def two(p, carry):
+            for half in range(2):
+                k = step * SWEEPS + 2 * p + 1 + half
+                sweep((cur, nxt)[half], (nxt, cur)[half], rhs, weights, low(k), high(k), 12)
+            return carry
+
+        lax.fori_loop(0, SWEEPS // 2, two, 0)
+
     limit = DEEP + ROWS
-    for s in range(1, DEEP + 1):
-        if s == DEEP // 2 + 1:
-            renew(s, limit - s)
-        sweep(buffers[(s - 1) % 2], buffers[s % 2], rhs, weights, s, limit - s, 12)
+    reach = lambda k: limit - k
+    sweeps(0, lambda k: k, reach)
+    relay_back()
+    renew(SWEEPS + 1, reach(SWEEPS + 1))
+    sweeps(1, lambda k: k, reach)
 
     wait_ways(0, range(5, 8))
-    for i in range(8, 10):
-        unpack(i)
-
-    @pl.when(top)
+
+    @pl.when(has_n)
     def _():
-        wait_fold(0)
-
-        def ghost(d, carry):
-            tiles = mirrored(lambda p: fold[p, DEEP - 1 - d], CP)
-            for t in range(3):
-                cur[t, limit + d] = tiles[t]
-            return carry
-
-        lax.fori_loop(0, DEEP, ghost, 0)
-
+        for i in range(8, 10):
+            unpack(i)
+
+    relay_end()
     lax.fori_loop(limit, EXT, begin_ghost, 0)
-    for s in range(1, DEEP + 1):
-        if s == DEEP // 2 + 1:
-            renew(limit - s, EXT - s)
-        sweep(buffers[(s - 1) % 2], buffers[s % 2], rhs, weights, limit - s, EXT - s, 12)
-
-    for b in range(0, BAND, 2):
-        for half in range(2):
-            for t in range(2):
-                rows = []
-                for row in (2 * b + half, 2 * b + 2 + half):
-                    value = cur[t, row + DEEP] * sigma
-                    state_ref[t, row] = value
-                    rows.append(value)
-                rows = jnp.concatenate(rows, axis=0)
-                high = rows.astype(BF16)
-                low = (rows - high.astype(F32)).astype(BF16)
+    sweeps(0, reach, lambda k: EXT - k)
+    renew(reach(SWEEPS + 1), EXT - SWEEPS - 1)
+    sweeps(1, reach, lambda k: EXT - k)
+
+    for b in range(0, BAND, 4):
+        for t in range(2):
+            values = [cur[t, 2 * b + k + DEEP] * sigma for k in range(8)]
+            across = jnp.swapaxes(jnp.stack(values, axis=0), 0, 1)
+            state_ref[:, 2 * b : 2 * b + 8, t * 128 : (t + 1) * 128] = across[:C]
+            for half in range(2):
                 first = half * COLS + t * 128
-                pieces[b * CP : (b + 2) * CP, first : first + 128] = high
-                pieces[b * CP : (b + 2) * CP, PLACES + first : PLACES + first + 128] = low
-
-    def chunk(g, carry):
-        bands = []
+                for k in range(2):
+                    rows = jnp.concatenate([values[4 * k + half], values[4 * k + 2 + half]], axis=0)
+                    high = rows.astype(BF16)
+                    low = (rows - high.astype(F32)).astype(BF16)
+                    here = pl.ds((b + 2 * k) * CP, 2 * CP)
+                    pieces[here, first : first + 128] = high
+                    pieces[here, PLACES + first : PLACES + first + 128] = low
+
+    def multiply(g, onehot, picked):
         for j in range(back):
-            band, halves = split(arrived[g * back + j, C : C + 1, :])
-            bands.append(band)
-            store_onehot(onehot0, halves, slice(j * 128, (j + 1) * 128))
-        hot = onehot0[:, : back * 128]
-        picked = jnp.dot(pieces[:, :PLACES], hot, preferred_element_type=F32) + jnp.dot(
+            _, halves = split(arrived[g * back + j, C : C + 1, :])
+            store_onehot(onehot, halves, slice(j * 128, (j + 1) * 128))
+        hot = onehot[:, : back * 128]
+        picked[...] = jnp.dot(pieces[:, :PLACES], hot, preferred_element_type=F32) + jnp.dot(
             pieces[:, PLACES:], hot, preferred_element_type=F32
         )
+
+    def pick(g, picked):
         for j in range(back):
-            band = jnp.broadcast_to(bands[j], (CP, 128))
+            band, _ = split(arrived[g * back + j, C : C + 1, :])
+            band = jnp.broadcast_to(band, (CP, 128))
             fit = jnp.zeros((CP, 128), F32)
             for b in range(BAND):
                 fit += jnp.where(band == b, picked[b * CP : (b + 1) * CP, j * 128 : (j + 1) * 128], 0.0)
             fits[g * back + j] = fit
-        for j in range(back):
-            i = g * back + j
-            to = lax.rem(me - i + n, n)
-
-            @pl.when(i > 0)
-            def _():
-                pltpu.make_async_remote_copy(
-                    src_ref=fits.at[i, 0:C, :],
-                    dst_ref=out_ref.at[:, me, :],
-                    send_sem=back_send,
-                    recv_sem=back_recv,
-                    device_id=place_of(to, n_lon),
-                    device_id_type=MESH,
-                ).start()
-
-        return carry
-
-    lax.fori_loop(0, n // back, chunk, 0)
+
+    def give_back(i):
+        pltpu.make_async_remote_copy(
+            src_ref=fits.at[i, 0:C, :],
+            dst_ref=out_ref.at[:, me, :],
+            send_sem=back_send,
+            recv_sem=back_recv,
+            device_id=place_of(lax.rem(me - i + n, n), n_lon),
+            device_id_type=MESH,
+        ).start()
+
+    def hand(g):
+        @pl.when(g > 0)
+        def _():
+            give_back(g * back)
+
+        for j in range(1, back):
+            give_back(g * back + j)
+
+    multiply(0, onehot0, picked0)
+
+    def turn(i, carry):
+        multiply(2 * i + 1, onehot1, picked1)
+        pick(2 * i, picked0)
+        multiply(2 * i + 2, onehot0, picked0)
+        pick(2 * i + 1, picked1)
+        hand(2 * i)
+        hand(2 * i + 1)
+        return carry
+
+    turns = n // back // 2
+    lax.fori_loop(0, turns - 1, turn, 0)
+    multiply(2 * turns - 1, onehot1, picked1)
+    pick(2 * turns - 2, picked0)
+    hand(2 * turns - 2)
+    pick(2 * turns - 1, picked1)
+    hand(2 * turns - 1)
     own_fit = pltpu.make_async_copy(fits.at[0, 0:C, :], out_ref.at[:, me, :], local_sem.at[0])
     own_fit.start()
     own_fit.wait()
@@ -517,10 +638,11 @@
     pltpu.make_async_copy(sent, sent, back_recv).wait()
 
 
-def run(n_lat, n_lon, partner, value, cell, coef, scale, sigma):
+def run(n_lat, n_lon, partner, count, scale, sigma, value, cell, bottom_level, diffusivity):
     n = n_lat * n_lon
     size = min(8, n // 4)
     back = min(4, n // 4)
+    planes = n_lat // 2
     vmem = pl.BlockSpec(memory_space=pltpu.VMEM)
     buffers = [
         pltpu.VMEM((BAND * 2 * CP, size * 128), BF16),
@@ -531,12 +653,11 @@
         functools.partial(kernel, n_lat, n_lon, size, back),
         out_shape=(
             jax.ShapeDtypeStruct((C, n, 128), F32),
-            jax.ShapeDtypeStruct((2, ROWS, CP, 128), F32),
+            jax.ShapeDtypeStruct((C, ROWS, COLS), F32),
         ),
         in_specs=[
-            pl.BlockSpec(memory_space=pltpu.SMEM),
+            *[pl.BlockSpec(memory_space=pltpu.SMEM)] * 4,
             pl.BlockSpec(memory_space=pl.ANY),
-            vmem,
             vmem,
             vmem,
             vmem,
@@ -551,6 +672,9 @@
             pltpu.VMEM((2, ROWS, CP, 128), F32),
             pltpu.VMEM((n, CP, 128), F32),
             pltpu.VMEM((BAND * CP, 2 * PLACES), BF16),
+            pltpu.VMEM((BAND * CP, back * 128), F32),
+            pltpu.VMEM((BAND * CP, back * 128), F32),
+            pltpu.VMEM((2, 3, ROWS, 128), F32),
             *[state] * 8,
             pltpu.VMEM((ROWS // 8, CP, 128), F32),
             pltpu.VMEM((ROWS // 8, CP, 128), F32),
@@ -559,15 +683,18 @@
             pltpu.VMEM((2, 3, CEXT, 128), F32),
             pltpu.VMEM((3, CEXT, 128), F32),
             pltpu.VMEM((3, CEXT, 128), F32),
-            pltpu.VMEM((2 * n_lon, DEEP, CP, 128), F32),
+            pltpu.VMEM((2 * n_lon, DEEP // planes, CP, 128), F32),
             pltpu.VMEM((2 * n_lon, 3, GRP, 128), F32),
+            pltpu.VMEM((3, DEEP // planes, CP, 128), F32),
             pltpu.SemaphoreType.DMA((2,)),
             pltpu.SemaphoreType.DMA,
-            pltpu.SemaphoreType.DMA((n // size,)),
+            pltpu.SemaphoreType.DMA((n // size // 2,)),
             pltpu.SemaphoreType.DMA((8, 2)),
             pltpu.SemaphoreType.DMA((8, 2)),
             pltpu.SemaphoreType.DMA((2, n_lon)),
             pltpu.SemaphoreType.DMA((2, n_lon)),
+            pltpu.SemaphoreType.DMA((2, planes)),
+            pltpu.SemaphoreType.DMA((2, planes)),
             pltpu.SemaphoreType.DMA,
             pltpu.SemaphoreType.DMA,
         ],
@@ -575,22 +702,15 @@
             collective_id=0, has_side_effects=True, vmem_limit_bytes=VMEM_LIMIT
         ),
         name="covariance",
-    )(partner, value, cell, coef, scale, sigma)
+    )(partner, count, scale, sigma, value, cell, bottom_level, diffusivity)
 
 
 def per_device(
     n_lat, n_lon, obs_value, obs_cell, obs_count, bottom_level, diffusivity, partner, length_scale, sigma
 ):
-    n = n_lat * n_lon
-    slots = lax.broadcasted_iota(jnp.int32, (n, 128), 1)
-    cell = jnp.where(slots < obs_count[0][:, None], obs_cell[0], -1).astype(F32)
-    coef = jnp.concatenate([bottom_level.astype(F32)[None], diffusivity], axis=0)
-    coef = coef.reshape(3, ROWS, 2, 128).transpose(2, 0, 1, 3)
-    column = lambda x: jnp.pad(x, (0, CP - C))[:, None]
-    fit, state = run(
-        n_lat, n_lon, partner, obs_value[0], cell, coef, column(length_scale), column(sigma)
+    fit, diffused = run(
+        n_lat, n_lon, partner, obs_count, length_scale, sigma, obs_value[0], obs_cell[0], bottom_level, diffusivity
     )
-    diffused = state[:, :, :C, :].transpose(2, 1, 0, 3).reshape(C, ROWS, COLS)
     return fit[None], diffused
 
 

time: 185 us -> 132 us (0.71)
  Pallas kernels: 173 us -> 128 us
  local copies, waits for them, and re-layouts: 7.77 us -> 3.61 us
  other arithmetic: 3.06 us -> 0 us
    pallas_call x1, Pallas kernels: 173 us -> 128 us  [run(): pl.pallas_call(functools.partial(kernel, n_lat, n_lon, size, back), out_s...]
    broadcast_in_dim x4 -> x0, local copies, waits for them, and re-layouts: 2.68 us -> none  [per_device(): column = lambda x: jnp.pad(x, (0, CP - C))[:, None]]
    unnamed x5 -> x4, local copies, waits for them, and re-layouts: 1.11 us -> 3.61 us
    convert_element_type x2 -> x0, other arithmetic: 2.39 us -> none  [the longest x1 1.56 us: per_device(): cell = jnp.where(slots < obs_count[0][:, None], obs_cell[0], -1).astype(F32)]
    transpose x2 -> x0, local copies, waits for them, and re-layouts: 2.15 us -> none  [per_device(): diffused = state[:, :, :C, :].transpose(2, 1, 0, 3).reshape(C, ROWS, COLS)]
where the time goes in v3:
time: 132 us
  Pallas kernels  128 us (97%)
  local copies, waits for them, and re-layouts  3.61 us (3%)
    pallas_call x1, Pallas kernels, run(): pl.pallas_call(functools.partial(kernel, n_lat, n_lon, size, back), out_s...  128 us
    unnamed x4, local copies, waits for them, and re-layouts  3.61 us

profile of v3, /device:TPU:0, one launch (start us, length us, event | category | flops | bytes accessed | tf_op | source)
XLA Modules:
  0.0 132.3 jit_solution(443859911656539417)
XLA Ops:
  0.6 128.0 %covariance.1 = (f32[21,128,128]{2,1,0:T(8,128)}, f32[21,48,256]{2,1,0:T(8,128)}) custom-call(s32[256]{0:T(256)} %partner_ref.1, s32[1,128]{1,0:T(1,128)} %count_ref.1, f32[21]{0:T(128)} %scale_ref.1, f32[21]{0:T(128)} %sigma_ref.1, f32[21,128,128]{2,1,0:T(8,128)} %bitcast.3, s32[128,128]{1,0:T(8,128)} %bitcast.5, s32[48,256]{1,0:T(8,128)} %bottom_ref.1, ...), custom_call_target="tpu_custom_call" | custom-call | tf_op jit(solution)/shard_map/covariance/pallas_call | solution.py:652
  128.7 0.0 copy-start
  128.7 2.6 %copy.12 = f32[1,21,128,128]{3,2,1,0:T(8,128)} copy(f32[1,21,128,128]{3,2,1,0:T(8,128)} %bitcast.4) | data formatting | bytes 2752512
  131.3 0.0 copy-done
  131.3 1.0 copy.13
Async XLA Ops:
  128.7 2.7 %copy-start = (f32[21,48,256]{2,1,0:T(8,128)S(1)}, f32[21,48,256]{2,1,0:T(8,128)}, u32[]{:S(2)}) copy-start(f32[21,48,256]{2,1,0:T(8,128)} %get-tuple-element.9) | copy-start | bytes 3096580
